TPU v7x, 512 devices: a whole 4x4x16 slice. The times are simulated.
512 devices in a mesh: ctx: 64 (over z_hi, y, x, core), tp: 8 (over z_lo).
Axes of the slice: x: 4, y: 4, z: 16 (z_hi: 2, z_lo: 8; z = z_hi * 8 + z_lo), core: 2. Of those that a mesh axis runs over, the one named last changes fastest.
Arguments:
- tokens: bfloat16 [16384, 4096], P('ctx', 'tp'), may hold values from -6 to 6
- norm_gain: bfloat16 [4096], P('tp'), may hold values from 0.25 to 1.75
- doc_ids: int32 [16384], P('ctx'), may hold values from 0 to 15, never falling along the last dimension, each value on 1 to 3840 neighbouring positions
- q_weight: bfloat16 [4096, 4096], P('ctx', 'tp'), may hold values from -0.09375 to 0.09375
- k_weight: bfloat16 [4096, 1024], P('ctx', 'tp'), may hold values from -0.09375 to 0.09375
- v_weight: bfloat16 [4096, 1024], P('ctx', 'tp'), may hold values from -0.09375 to 0.09375
- o_weight: bfloat16 [4096, 4096], P('tp', 'ctx'), may hold values from -0.09375 to 0.09375
Outputs:
- mixed: bfloat16 [16384, 4096], P('ctx', 'tp')
Inputs may be any that keep to these rules, and one draw needn't show every extreme that they name: `doc_ids`: non-decreasing along the sequence; each document is a run of at most 3840 tokens and one run has exactly 3840.
All inputs are finite; a program needn't handle non-finite values.
Results may differ from a plain program's by a relative error of at most 0.015.
Values may be sent and summed in bfloat16 or wider, within the bound.
No kernel may reach another device: no remote copies, remote signals or barrier semaphores. Data moves between devices by JAX's collectives and lax.ppermute only.
A program may use at most 64 MiB of HBM per device.

v0:
```python
import jax
import jax.numpy as jnp
from jax import lax
from jax.experimental import pallas as pl
from jax.experimental.pallas import tpu as pltpu
from jax.sharding import Mesh, PartitionSpec as P


HEAD = 128
PLANE = ("y", "x", "core")


def line(size, step):
    return [(i, i + step) for i in range(size) if 0 <= i + step < size]


def ring(size, step):
    return [(i, (i + step) % size) for i in range(size)]


def plane_route(step, first):
    route = []
    for y in range(4):
        for x in range(4):
            for core in range(2):
                if (core == 0) == first:
                    to = (y * 4 + (x + step) % 4) * 2 + core
                else:
                    to = ((y + step) % 4 * 4 + x) * 2 + core
                route.append(((y * 4 + x) * 2 + core, to))
    return route


def block_rows(where, core, e, d, z):
    zh, y, x = where[0], where[1], where[2]
    far, near = (4 - e) % 4, (4 - d) % 4
    at_y = (y + jnp.where(core == 0, far, near)) % 4
    at_x = (x + jnp.where(core == 0, near, far)) % 4
    at_zh = jnp.where(zh == z, 0, 1)
    return pl.multiple_of((((at_zh * 4 + at_y) * 4 + at_x) * 2 + core) * 64, 64)


def load_weights(where, pieces, buffer, sem, first_col):
    cols = buffer.shape[1]
    copies = []
    for n, piece in enumerate(pieces):
        core = jnp.where(n < 4, where[3], 1 - where[3])
        for d in range(4):
            for z in range(2):
                rows = block_rows(where, core, n % 4, d, z)
                copies.append(
                    pltpu.make_async_copy(
                        piece.at[d, z, :, pl.ds(first_col, cols)], buffer.at[pl.ds(rows, 64)], sem.at[0]
                    )
                )
    for copy in copies:
        copy.start()
    return copies


def turn(values, cos_ref, sin_ref):
    return values * cos_ref[...] + pltpu.roll(values, HEAD // 2, 1) * sin_ref[...]


def kv_kernel(where, x_ref, docs_ref, cos_ref, sin_ref, *rest):
    pieces, (tile_ref, normed_ref, buffer, sem) = rest[:8], rest[8:]
    copies = load_weights(where, pieces, buffer, sem, 512)
    n_tp, _, cols = x_ref.shape
    rows = normed_ref.shape[0]
    square = jnp.zeros((rows, cols), jnp.float32)
    for j in range(n_tp):
        block = x_ref[j, :rows].astype(jnp.float32)
        square = square + block * block
    scale = lax.rsqrt(jnp.sum(square, axis=1, keepdims=True) / (n_tp * cols) + 1e-05)
    for j in range(n_tp):
        block = x_ref[j, :rows].astype(jnp.float32)
        gain = x_ref[j, pl.ds(rows, 1)].astype(jnp.float32)
        normed_ref[:, j * cols : (j + 1) * cols] = (block * scale * gain).astype(jnp.bfloat16)
    for copy in copies:
        copy.wait()
    out = jnp.dot(normed_ref[...], buffer[...], preferred_element_type=jnp.float32)
    tile_ref[:rows, :HEAD] = turn(out[:, :HEAD], cos_ref, sin_ref).astype(jnp.bfloat16)
    tile_ref[:rows, HEAD:] = out[:, HEAD:].astype(jnp.bfloat16)
    tile_ref[rows:, :] = docs_ref[...]


def q_kernel(where, normed_ref, cos_ref, sin_ref, *rest):
    pieces, (q_ref, buffer, sem) = rest[:8], rest[8:]
    copies = load_weights(where, pieces, buffer, sem, 0)
    for copy in copies:
        copy.wait()
    out = jnp.dot(normed_ref[...], buffer[...], preferred_element_type=jnp.float32)
    factor = 1.4426950408889634 / HEAD**0.5
    for g in range(q_ref.shape[0]):
        head = turn(out[:, g * HEAD : (g + 1) * HEAD], cos_ref, sin_ref)
        q_ref[g] = (head * factor).astype(jnp.bfloat16)


def attention_kernel(q_ref, docs_ref, mine_ref, other_ref, out_ref, scores):
    group, rows, head = q_ref.shape
    q_docs = docs_ref[...]
    ones = jnp.ones((8, rows, head), jnp.bfloat16)
    for g in range(group):
        at = slice(g * rows, (g + 1) * rows)
        top = None
        for n in range(16):
            ref, s = (mine_ref, n) if n < 8 else (other_ref, n - 8)
            part = lax.dot_general(
                q_ref[g],
                ref[s, :rows, :head],
                (((1,), (1,)), ((), ())),
                preferred_element_type=jnp.float32,
            )
            allowed = ref[s, pl.ds(rows, 1), :].astype(jnp.float32) == q_docs
            if n == 7:
                q_at = lax.broadcasted_iota(jnp.int32, (rows, rows), 0)
                k_at = lax.broadcasted_iota(jnp.int32, (rows, rows), 1)
                allowed = allowed & (k_at <= q_at)
            part = jnp.where(allowed, part, -1e30)
            scores[at, n * rows : (n + 1) * rows] = part
            most = jnp.maximum(part[:, :head], part[:, head:])
            top = most if top is None else jnp.maximum(top, most)
        top = jnp.max(top, axis=1, keepdims=True)
        expw = jnp.exp2(scores[at, :] - top).astype(jnp.bfloat16)
        summed = jnp.zeros((rows, 2 * head), jnp.float32)
        for n, ref in enumerate((mine_ref, other_ref)):
            values = jnp.concatenate([ref[:, :rows, head:], ones], axis=2)
            values = values.reshape(8 * rows, 2 * head)
            summed = summed + jnp.dot(
                expw[:, n * 8 * rows : (n + 1) * 8 * rows], values, preferred_element_type=jnp.float32
            )
        out_ref[:, g * head : (g + 1) * head] = (summed[:, :head] / summed[:, head:]).astype(
            jnp.bfloat16
        )


def out_kernel(zh, a_ref, o_ref, out_ref):
    del zh
    for j in range(o_ref.shape[0]):
        out_ref[j] = lax.dot_general(
            a_ref[...], o_ref[j], (((1,), (1,)), ((), ())), preferred_element_type=jnp.float32
        ).astype(jnp.bfloat16)


def local(tokens, norm_gain, doc_ids, q_weight, k_weight, v_weight, o_weight):
    rows, cols = tokens.shape
    n_tp = lax.axis_size("tp")
    q_cols = q_weight.shape[1]
    kv_cols = k_weight.shape[1]
    group = q_cols // HEAD
    zh, y, x, core = (lax.axis_index(a) for a in ("zh", "y", "x", "core"))
    shard = ((zh * 4 + y) * 4 + x) * 2 + core
    where = jnp.stack([zh, y, x, core]).astype(jnp.int32)
    swap = [(0, 1), (1, 0)]

    block = jnp.concatenate([tokens, jnp.broadcast_to(norm_gain[None], (8, cols))], axis=0)
    whole = lax.all_gather(block, "tp", axis=0, tiled=False)

    weight = jnp.concatenate([q_weight, k_weight, v_weight], axis=1)
    away = lax.ppermute(weight, "zh", swap)
    pair = jnp.stack([weight, away])
    near = [pair] + [lax.ppermute(pair, PLANE, plane_route(d, True)) for d in range(1, 4)]
    near = jnp.stack(near)
    pieces = [near] + [lax.ppermute(near, PLANE, plane_route(e, False)) for e in range(1, 4)]

    o_block = o_weight.T
    o_away = lax.ppermute(o_block, "zh", swap)
    o_pair = jnp.stack([o_block, o_away])
    pieces = pieces + [lax.ppermute(piece, "core", swap) for piece in pieces]
    o_rows = lax.all_gather(o_pair, PLANE, axis=1, tiled=True)
    o_rows = o_rows.reshape(n_tp, cols, q_cols)

    inv_freq = 500000.0 ** (-(jnp.arange(HEAD // 2, dtype=jnp.float32) * 2.0) / HEAD)
    positions = (shard * rows + jnp.arange(rows, dtype=jnp.int32)).astype(jnp.float32)
    angles = positions[:, None] * inv_freq[None, :]
    cos_part, sin_part = jnp.cos(angles), jnp.sin(angles)
    cos_part = jnp.concatenate([cos_part, cos_part], axis=1)
    sin_part = jnp.concatenate([-sin_part, sin_part], axis=1)
    docs = doc_ids.astype(jnp.float32) + 1.0
    docs_rows = jnp.broadcast_to(docs[None].astype(jnp.bfloat16), (8, rows))

    vmem, hbm, smem = (pl.BlockSpec(memory_space=s) for s in (pltpu.VMEM, pl.ANY, pltpu.SMEM))
    tile, normed = pl.pallas_call(
        kv_kernel,
        out_shape=(
            jax.ShapeDtypeStruct((rows + 8, 2 * kv_cols), jnp.bfloat16),
            jax.ShapeDtypeStruct((rows, n_tp * cols), jnp.bfloat16),
        ),
        in_specs=[smem, vmem, vmem, vmem, vmem] + [hbm] * 8,
        scratch_shapes=[
            pltpu.VMEM((n_tp * cols, 2 * kv_cols), jnp.bfloat16),
            pltpu.SemaphoreType.DMA((1,)),
        ],
        name="kv_projection",
    )(where, whole, docs_rows, cos_part, sin_part, *pieces)
    q_rot = pl.pallas_call(
        q_kernel,
        out_shape=jax.ShapeDtypeStruct((group, rows, HEAD), jnp.bfloat16),
        in_specs=[smem, vmem, vmem, vmem] + [hbm] * 8,
        scratch_shapes=[
            pltpu.VMEM((n_tp * cols, q_cols), jnp.bfloat16),
            pltpu.SemaphoreType.DMA((1,)),
        ],
        cost_estimate=pl.CostEstimate(
            flops=2 * rows * n_tp * cols * q_cols, bytes_accessed=2 * n_tp * cols * (q_cols + rows), transcendentals=0
        ),
        name="q_projection",
    )(where, normed, cos_part, sin_part, *pieces)

    back_1 = lax.ppermute(tile, ("zh", "y"), line(8, 1))
    back_2 = lax.ppermute(tile, ("zh", "y"), line(8, 2))
    back_1, back_2, q_rot = lax.optimization_barrier((back_1, back_2, q_rot))
    mine = []
    for step in range(1, 4):
        two = jnp.stack([back_1, jnp.where(x + step < 4, tile, back_2)])
        mine.append(lax.ppermute(two, "x", ring(4, step)))
    sent = mine + [jnp.stack([back_1, jnp.where(core == 0, tile, back_2)])]
    other = lax.ppermute(jnp.concatenate(sent), "core", swap)
    mine = jnp.concatenate(mine + [jnp.stack([back_1, tile])])

    attended = pl.pallas_call(
        attention_kernel,
        out_shape=jax.ShapeDtypeStruct((rows, q_cols), jnp.bfloat16),
        in_specs=[vmem] * 4,
        scratch_shapes=[pltpu.VMEM((group * rows, 16 * rows), jnp.float32)],
        name="attention",
    )(q_rot, docs[:, None], mine, other)

    half = n_tp // 2
    partial_terms = pl.pallas_call(
        out_kernel,
        out_shape=jax.ShapeDtypeStruct((n_tp, rows, cols), jnp.bfloat16),
        grid_spec=pltpu.PrefetchScalarGridSpec(
            num_scalar_prefetch=1,
            grid=(2,),
            in_specs=[
                pl.BlockSpec((rows, q_cols), lambda i, zh: (0, 0)),
                pl.BlockSpec((half, cols, q_cols), lambda i, zh: ((i + zh[0]) % 2, 0, 0)),
            ],
            out_specs=pl.BlockSpec((half, rows, cols), lambda i, zh: (i, 0, 0)),
        ),
        name="out_projection",
    )(where[:1], attended, o_rows)
    return lax.psum_scatter(
        partial_terms.reshape(n_tp * rows, cols), "tp", scatter_dimension=0, tiled=True
    )


def solution(mesh):
    fine = Mesh(mesh.devices.reshape(2, 4, 4, 2, 8), ("zh", "y", "x", "core", "tp"))
    ctx = ("zh", "y", "x", "core")
    return jax.shard_map(
        local,
        mesh=fine,
        in_specs=(
            P(ctx, "tp"),
            P("tp"),
            P(ctx),
            P(ctx, "tp"),
            P(ctx, "tp"),
            P(ctx, "tp"),
            P("tp", ctx),
        ),
        out_specs=P(ctx, "tp"),
        check_vma=False,
    )
```

profile of v0, /device:TPU:6, one launch (start us, length us, event | category | flops | bytes accessed | tf_op | source)
XLA Modules:
  0.0 269.2 jit_solution(10643185432247659869)
XLA Ops:
  6.5 0.7 broadcast_in_dim.6
  7.3 1.7 pad_maximum_fusion.4
  9.0 15.7 %collective-permute-start.17 = (bf16[64,512]{1,0:T(8,128)(2,1)}, bf16[64,512]{1,0:T(8,128)(2,1)S(1)}, u32[]{:S(2)}, u32[]{:S(2)}) collective-permute-start(bf16[64,512]{1,0:T(8,128)(2,1)} %bitcast.41), channel_id=1, source_target_pairs={{0,256},{256,0},{1,257},{257,1},{2,258},{258,2},{3,259},{259,3},{4... | collective-permute-start | bytes 196616 | tf_op jit(solution)/shard_map/ppermute | solution.py:167
  24.8 4.5 %collective-permute-done.17 = bf16[64,512]{1,0:T(8,128)(2,1)S(1)} collective-permute-done((bf16[64,512]{1,0:T(8,128)(2,1)}, bf16[64,512]{1,0:T(8,128)(2,1)S(1)}, u32[]{:S(2)}, u32[]{:S(2)}) %collective-permute-start.17) | collective-permute-done | bytes 65568 | tf_op jit(solution)/shard_map/ppermute | solution.py:167
  29.3 1.5 pad_maximum_fusion.8
  30.9 13.0 %collective-permute-start = (bf16[64,768]{1,0:T(8,128)(2,1)S(1)}, bf16[64,768]{1,0:T(8,128)(2,1)S(1)}, u32[]{:S(2)}, u32[]{:S(2)}) collective-permute-start(bf16[64,768]{1,0:T(8,128)(2,1)S(1)} %constant_dynamic-update-slice_fusion), channel_id=1, source_target_pairs={{0,256},{256,0},{1,257},{257,1},{2,258},{258,2},{3,259},{259,3},{4... | collective-permute-start | bytes 294920 | tf_op jit(solution)/shard_map/ppermute | solution.py:160
  43.9 6.3 %collective-permute-done = bf16[64,768]{1,0:T(8,128)(2,1)S(1)} collective-permute-done((bf16[64,768]{1,0:T(8,128)(2,1)S(1)}, bf16[64,768]{1,0:T(8,128)(2,1)S(1)}, u32[]{:S(2)}, u32[]{:S(2)}) %collective-permute-start) | collective-permute-done | bytes 98336 | tf_op jit(solution)/shard_map/ppermute | solution.py:160
  50.2 2.7 %collective-permute-start.3 = (bf16[2,64,768]{2,1,0:T(8,128)(2,1)S(1)}, bf16[2,64,768]{2,1,0:T(8,128)(2,1)S(1)}, u32[]{:S(2)}, u32[]{:S(2)}) collective-permute-start(bf16[2,64,768]{2,1,0:T(8,128)(2,1)S(1)} %get-tuple-element.19), channel_id=1, source_target_pairs={{0,48},{8,200},{16,0},{24,216},{32,16},{40,232},{48,32},{56,248},{... | collective-permute-start | bytes 589832 | tf_op jit(solution)/shard_map/ppermute | solution.py:162
  53.0 4.3 %collective-permute-start.1 = (bf16[2,64,768]{2,1,0:T(8,128)(2,1)S(1)}, bf16[2,64,768]{2,1,0:T(8,128)(2,1)S(1)}, u32[]{:S(2)}, u32[]{:S(2)}) collective-permute-start(bf16[2,64,768]{2,1,0:T(8,128)(2,1)S(1)} %get-tuple-element.19), channel_id=1, source_target_pairs={{0,16},{8,72},{16,32},{24,88},{32,48},{40,104},{48,0},{56,120},{64... | collective-permute-start | bytes 589832 | tf_op jit(solution)/shard_map/ppermute | solution.py:162
  57.3 2.1 collective-permute-start.2
  59.4 1.1 collective-permute-done.1
  60.5 7.9 %collective-permute-done.2 = bf16[2,64,768]{2,1,0:T(8,128)(2,1)S(1)} collective-permute-done((bf16[2,64,768]{2,1,0:T(8,128)(2,1)S(1)}, bf16[2,64,768]{2,1,0:T(8,128)(2,1)S(1)}, u32[]{:S(2)}, u32[]{:S(2)}) %collective-permute-start.2) | collective-permute-done | bytes 196640 | tf_op jit(solution)/shard_map/ppermute | solution.py:162
  68.5 0.1 pad_maximum_fusion.rest_0_
  68.6 5.0 %collective-permute-start.6 = (bf16[4,2,64,768]{3,2,1,0:T(8,128)(2,1)S(1)}, bf16[4,2,64,768]{3,2,1,0:T(8,128)(2,1)S(1)}, u32[]{:S(2)}, u32[]{:S(2)}) collective-permute-start(bf16[4,2,64,768]{3,2,1,0:T(8,128)(2,1)S(1)} %pad_maximum_fusion.rest_0_), channel_id=1, source_target_pairs={{0,192},{8,56},{16,208},{24,8},{32,224},{40,24},{48,240},{56,40},{... | collective-permute-start | bytes 2359304 | tf_op jit(solution)/shard_map/ppermute | solution.py:164
  73.6 1.9 collective-permute-start.4
  75.5 4.1 %collective-permute-start.5 = (bf16[4,2,64,768]{3,2,1,0:T(8,128)(2,1)S(1)}, bf16[4,2,64,768]{3,2,1,0:T(8,128)(2,1)S(1)}, u32[]{:S(2)}, u32[]{:S(2)}) collective-permute-start(bf16[4,2,64,768]{3,2,1,0:T(8,128)(2,1)S(1)} %pad_maximum_fusion.rest_0_), channel_id=1, source_target_pairs={{0,128},{8,40},{16,144},{24,56},{32,160},{40,8},{48,176},{56,24},{... | collective-permute-start | bytes 2359304 | tf_op jit(solution)/shard_map/ppermute | solution.py:164
  79.6 1.9 collective-permute-start.7
  81.6 9.9 %collective-permute-done.6.rest_3_ = bf16[4,2,64,768]{3,2,1,0:T(8,128)(2,1)S(1)} collective-permute-done((bf16[4,2,64,768]{3,2,1,0:T(8,128)(2,1)S(1)}, bf16[4,2,64,768]{3,2,1,0:T(8,128)(2,1)S(1)}, u32[]{:S(2)}, u32[]{:S(2)}) %collective-permute-start.6) | collective-permute-done | bytes 786464 | tf_op jit(solution)/shard_map/ppermute | solution.py:164
  91.5 1.9 collective-permute-start.10
  93.4 3.7 %collective-permute-done.4.rest_1_ = bf16[4,2,64,768]{3,2,1,0:T(8,128)(2,1)S(1)} collective-permute-done((bf16[4,2,64,768]{3,2,1,0:T(8,128)(2,1)S(1)}, bf16[4,2,64,768]{3,2,1,0:T(8,128)(2,1)S(1)}, u32[]{:S(2)}, u32[]{:S(2)}) %collective-permute-start.4) | collective-permute-done | bytes 786464 | tf_op jit(solution)/shard_map/ppermute | solution.py:164
  97.1 1.9 collective-permute-start.8
  99.0 2.4 collective-permute-start.9
  101.4 0.7 pad_add_fusion.where
  102.1 0.5 fusion
  102.7 0.8 pad_maximum_fusion.6
  103.6 0.9 copy-done.5
  104.4 0.2 copy-done.6
  104.7 0.9 copy-done.7
  105.6 0.6 broadcast_in_dim.7.docs_ref
  106.2 4.8 %kv_projection.1 = (bf16[264,256]{1,0:T(8,128)(2,1)}, bf16[256,4096]{1,0:T(8,128)(2,1)}) custom-call(s32[4]{0:T(128)} %pad_add_fusion.where, bf16[8,264,512]{2,1,0:T(8,128)(2,1)} %bitcast.34, bf16[8,256]{1,0:T(8,128)(2,1)} %broadcast_in_dim.7.docs_ref, f32[256,128]{1,0:T(8,128)} %get-tuple-element.28.cos_ref, f32[256,128]{1,0:T(8,128)} %get-tuple-element.29.sin_ref, ...), custom_call_target="tpu_custom_call" | custom-call | tf_op jit(solution)/shard_map/kv_projection/pallas_call | solution.py:183
  111.0 1.3 collective-permute-start.11
  112.3 3.9 %collective-permute-start.12 = (bf16[264,256]{1,0:T(8,128)(2,1)}, bf16[264,256]{1,0:T(8,128)(2,1)S(1)}, u32[]{:S(2)}, u32[]{:S(2)}) collective-permute-start(bf16[264,256]{1,0:T(8,128)(2,1)} %get-tuple-element.10), channel_id=1, source_target_pairs={{0,128},{64,192},{128,256},{192,320},{256,384},{320,448},{1,129},{... | collective-permute-start | bytes 405512 | tf_op jit(solution)/shard_map/ppermute | solution.py:211
  116.2 6.1 %q_projection.1.q_ref = bf16[4,256,128]{2,1,0:T(8,128)(2,1)} custom-call(s32[4]{0:T(128)} %pad_add_fusion.where, bf16[256,4096]{1,0:T(8,128)(2,1)} %get-tuple-element.11.normed_ref, f32[256,128]{1,0:T(8,128)} %get-tuple-element.28.cos_ref, f32[256,128]{1,0:T(8,128)} %get-tuple-element.29.sin_ref, bf16[4,2,64,768]{3,2,1,0:T(8,128)(2,1)} %copy-done, ...), custom_call_target="tpu_custom_call" | custom-call | flops 1073741824 | bytes 6291456 | tf_op jit(solution)/shard_map/q_projection/pallas_call | solution.py:196
  122.4 0.1 pad_maximum_fusion.1
  122.5 1.9 collective-permute-start.13
  124.4 1.9 collective-permute-start.14
  126.3 3.9 %collective-permute-start.15 = (bf16[2,264,256]{2,1,0:T(8,128)(2,1)S(1)}, bf16[2,264,256]{2,1,0:T(8,128)(2,1)S(1)}, u32[]{:S(2)}, u32[]{:S(2)}) collective-permute-start(bf16[2,264,256]{2,1,0:T(8,128)(2,1)S(1)} %get-tuple-element.20), channel_id=1, source_target_pairs={{0,48},{16,0},{32,16},{48,32},{1,49},{17,1},{33,17},{49,33},{2,50}... | collective-permute-start | bytes 811016 | tf_op jit(solution)/shard_map/ppermute | solution.py:216
  130.3 3.5 %collective-permute-done.13 = bf16[2,264,256]{2,1,0:T(8,128)(2,1)S(1)} collective-permute-done((bf16[2,264,256]{2,1,0:T(8,128)(2,1)S(1)}, bf16[2,264,256]{2,1,0:T(8,128)(2,1)S(1)}, u32[]{:S(2)}, u32[]{:S(2)}) %collective-permute-start.13) | collective-permute-done | bytes 270368 | tf_op jit(solution)/shard_map/ppermute | solution.py:216
  133.7 3.5 %collective-permute-done.14 = bf16[2,264,256]{2,1,0:T(8,128)(2,1)S(1)} collective-permute-done((bf16[2,264,256]{2,1,0:T(8,128)(2,1)S(1)}, bf16[2,264,256]{2,1,0:T(8,128)(2,1)S(1)}, u32[]{:S(2)}, u32[]{:S(2)}) %collective-permute-start.14) | collective-permute-done | bytes 270368 | tf_op jit(solution)/shard_map/ppermute | solution.py:216
  137.2 8.2 %collective-permute-done.15 = bf16[2,264,256]{2,1,0:T(8,128)(2,1)S(1)} collective-permute-done((bf16[2,264,256]{2,1,0:T(8,128)(2,1)S(1)}, bf16[2,264,256]{2,1,0:T(8,128)(2,1)S(1)}, u32[]{:S(2)}, u32[]{:S(2)}) %collective-permute-start.15) | collective-permute-done | bytes 270368 | tf_op jit(solution)/shard_map/ppermute | solution.py:216
  145.4 0.1 copy.15
  145.6 2.1 collective-permute-start.16
  147.7 0.8 copy.8.docs_ref
  148.5 1.9 collective-permute-done.16.other_ref
  150.4 1.0 copy-done.9
  151.3 9.1 %attention.1.a_ref = bf16[256,512]{1,0:T(8,128)(2,1)} custom-call(bf16[4,256,128]{2,1,0:T(8,128)(2,1)} %q_projection.1.q_ref, f32[256,1]{1,0:T(8,128)} %copy.8.docs_ref, bf16[8,264,256]{2,1,0:T(8,128)(2,1)} %copy-done.1, bf16[8,264,256]{2,1,0:T(8,128)(2,1)} %copy-done.9), custom_call_target="tpu_custom_call" | custom-call | tf_op jit(solution)/shard_map/attention/pallas_call | solution.py:221
  160.4 4.1 %out_projection.1 = bf16[8,256,512]{2,1,0:T(8,128)(2,1)} custom-call(s32[1]{0:T(128)} %bitcast.zh, bf16[256,512]{1,0:T(8,128)(2,1)} %attention.1.a_ref, bf16[8,512,512]{2,1,0:T(8,128)(2,1)} %bitcast.33), custom_call_target="tpu_custom_call" | custom-call | tf_op jit(solution)/shard_map/out_projection/pallas_call | solution.py:230
  164.5 98.1 %reduce-scatter.2.cloned.1.call-done = bf16[256,512]{1,0:T(8,128)(2,1)} async-done(((bf16[2048,512]{1,0:T(8,128)(2,1)}), bf16[256,512]{1,0:T(8,128)(2,1)}) %reduce-scatter.2.cloned.1.call-update) | async-done | bytes 262160 | tf_op jit(solution)/shard_map/reduce_scatter | solution.py:244
  (54 shorter events, 0.4 us)
Async XLA Ops:
  6.5 24.3 %copy-start.10 = (bf16[64,512]{1,0:T(8,128)(2,1)S(1)}, bf16[64,512]{1,0:T(8,128)(2,1)}, u32[]{:S(2)}) copy-start(bf16[64,512]{1,0:T(8,128)(2,1)} %param.10) | copy-start | bytes 196612
  6.5 24.3 %copy-start.11 = (bf16[64,128]{1,0:T(8,128)(2,1)S(1)}, bf16[64,128]{1,0:T(8,128)(2,1)}, u32[]{:S(2)}) copy-start(bf16[64,128]{1,0:T(8,128)(2,1)} %param.11) | copy-start | bytes 49156
  6.5 24.4 %copy-start.12 = (bf16[64,128]{1,0:T(8,128)(2,1)S(1)}, bf16[64,128]{1,0:T(8,128)(2,1)}, u32[]{:S(2)}) copy-start(bf16[64,128]{1,0:T(8,128)(2,1)} %param.12) | copy-start | bytes 49156
  6.5 99.0 %all-gather.6.cloned.1.call-start = ((), (), s32[]{:S(2)}) async-start(), calls=%async_computation.3 | async-start | bytes 2433024 | tf_op jit(solution)/shard_map/all_gather | solution.py:157
  9.0 151.4 %all-gather.4.cloned.1.call-start = ((), (), s32[]{:S(2)}) async-start(), calls=%async_computation.1 | async-start | bytes 4325376 | tf_op jit(solution)/shard_map/all_gather | solution.py:170
  9.0 20.3 %collective-permute-start.17 = (bf16[64,512]{1,0:T(8,128)(2,1)}, bf16[64,512]{1,0:T(8,128)(2,1)S(1)}, u32[]{:S(2)}, u32[]{:S(2)}) collective-permute-start(bf16[64,512]{1,0:T(8,128)(2,1)} %bitcast.41), channel_id=1, source_target_pairs={{0,256},{256,0},{1,257},{257,1},{2,258},{258,2},{3,259},{259,3},{4... | collective-permute-start | bytes 196616 | tf_op jit(solution)/shard_map/ppermute | solution.py:167
  30.8 231.8 %reduce-scatter.2.cloned.1.call-start = ((), (), s32[]{:S(2)}) async-start(), calls=%async_computation.2 | async-start | bytes 2359296 | tf_op jit(solution)/shard_map/reduce_scatter | solution.py:244
  30.9 19.3 %collective-permute-start = (bf16[64,768]{1,0:T(8,128)(2,1)S(1)}, bf16[64,768]{1,0:T(8,128)(2,1)S(1)}, u32[]{:S(2)}, u32[]{:S(2)}) collective-permute-start(bf16[64,768]{1,0:T(8,128)(2,1)S(1)} %constant_dynamic-update-slice_fusion), channel_id=1, source_target_pairs={{0,256},{256,0},{1,257},{257,1},{2,258},{258,2},{3,259},{259,3},{4... | collective-permute-start | bytes 294920 | tf_op jit(solution)/shard_map/ppermute | solution.py:160
  50.2 9.2 %collective-permute-start.3 = (bf16[2,64,768]{2,1,0:T(8,128)(2,1)S(1)}, bf16[2,64,768]{2,1,0:T(8,128)(2,1)S(1)}, u32[]{:S(2)}, u32[]{:S(2)}) collective-permute-start(bf16[2,64,768]{2,1,0:T(8,128)(2,1)S(1)} %get-tuple-element.19), channel_id=1, source_target_pairs={{0,48},{8,200},{16,0},{24,216},{32,16},{40,232},{48,32},{56,248},{... | collective-permute-start | bytes 589832 | tf_op jit(solution)/shard_map/ppermute | solution.py:162
  53.0 7.6 %collective-permute-start.1 = (bf16[2,64,768]{2,1,0:T(8,128)(2,1)S(1)}, bf16[2,64,768]{2,1,0:T(8,128)(2,1)S(1)}, u32[]{:S(2)}, u32[]{:S(2)}) collective-permute-start(bf16[2,64,768]{2,1,0:T(8,128)(2,1)S(1)} %get-tuple-element.19), channel_id=1, source_target_pairs={{0,16},{8,72},{16,32},{24,88},{32,48},{40,104},{48,0},{56,120},{64... | collective-permute-start | bytes 589832 | tf_op jit(solution)/shard_map/ppermute | solution.py:162
  57.3 11.2 %collective-permute-start.2 = (bf16[2,64,768]{2,1,0:T(8,128)(2,1)S(1)}, bf16[2,64,768]{2,1,0:T(8,128)(2,1)S(1)}, u32[]{:S(2)}, u32[]{:S(2)}) collective-permute-start(bf16[2,64,768]{2,1,0:T(8,128)(2,1)S(1)} %get-tuple-element.19), channel_id=1, source_target_pairs={{0,32},{8,136},{16,48},{24,152},{32,0},{40,168},{48,16},{56,184},{... | collective-permute-start | bytes 589832 | tf_op jit(solution)/shard_map/ppermute | solution.py:162
  68.5 35.0 %copy-start.13 = (s32[256]{0:T(256)S(1)}, s32[256]{0:T(256)}, u32[]{:S(2)}) copy-start(s32[256]{0:T(256)} %param.9) | copy-start | bytes 3076
  68.6 37.6 %copy-start = (bf16[4,2,64,768]{3,2,1,0:T(8,128)(2,1)}, bf16[4,2,64,768]{3,2,1,0:T(8,128)(2,1)S(1)}, u32[]{:S(2)}) copy-start(bf16[4,2,64,768]{3,2,1,0:T(8,128)(2,1)S(1)} %pad_maximum_fusion.rest_0_) | copy-start | bytes 2359300
  68.6 22.9 %collective-permute-start.6 = (bf16[4,2,64,768]{3,2,1,0:T(8,128)(2,1)S(1)}, bf16[4,2,64,768]{3,2,1,0:T(8,128)(2,1)S(1)}, u32[]{:S(2)}, u32[]{:S(2)}) collective-permute-start(bf16[4,2,64,768]{3,2,1,0:T(8,128)(2,1)S(1)} %pad_maximum_fusion.rest_0_), channel_id=1, source_target_pairs={{0,192},{8,56},{16,208},{24,8},{32,224},{40,24},{48,240},{56,40},{... | collective-permute-start | bytes 2359304 | tf_op jit(solution)/shard_map/ppermute | solution.py:164
  73.6 23.5 %collective-permute-start.4 = (bf16[4,2,64,768]{3,2,1,0:T(8,128)(2,1)S(1)}, bf16[4,2,64,768]{3,2,1,0:T(8,128)(2,1)S(1)}, u32[]{:S(2)}, u32[]{:S(2)}) collective-permute-start(bf16[4,2,64,768]{3,2,1,0:T(8,128)(2,1)S(1)} %pad_maximum_fusion.rest_0_), channel_id=1, source_target_pairs={{0,64},{8,24},{16,80},{24,40},{32,96},{40,56},{48,112},{56,8},{64,... | collective-permute-start | bytes 2359304 | tf_op jit(solution)/shard_map/ppermute | solution.py:164
  75.5 23.5 %collective-permute-start.5 = (bf16[4,2,64,768]{3,2,1,0:T(8,128)(2,1)S(1)}, bf16[4,2,64,768]{3,2,1,0:T(8,128)(2,1)S(1)}, u32[]{:S(2)}, u32[]{:S(2)}) collective-permute-start(bf16[4,2,64,768]{3,2,1,0:T(8,128)(2,1)S(1)} %pad_maximum_fusion.rest_0_), channel_id=1, source_target_pairs={{0,128},{8,40},{16,144},{24,56},{32,160},{40,8},{48,176},{56,24},{... | collective-permute-start | bytes 2359304 | tf_op jit(solution)/shard_map/ppermute | solution.py:164
  79.6 23.9 %collective-permute-start.7 = (bf16[4,2,64,768]{3,2,1,0:T(8,128)(2,1)S(1)}, bf16[4,2,64,768]{3,2,1,0:T(8,128)(2,1)S(1)}, u32[]{:S(2)}, u32[]{:S(2)}) collective-permute-start(bf16[4,2,64,768]{3,2,1,0:T(8,128)(2,1)S(1)} %pad_maximum_fusion.rest_0_), channel_id=1, source_target_pairs={{0,8},{8,0},{1,9},{9,1},{2,10},{10,2},{3,11},{11,3},{4,12},{12,4},... | collective-permute-start | bytes 2359304 | tf_op jit(solution)/shard_map/ppermute | solution.py:169
  91.5 14.7 %copy-start.2 = (bf16[4,2,64,768]{3,2,1,0:T(8,128)(2,1)}, bf16[4,2,64,768]{3,2,1,0:T(8,128)(2,1)S(1)}, u32[]{:S(2)}) copy-start(bf16[4,2,64,768]{3,2,1,0:T(8,128)(2,1)S(1)} %collective-permute-done.6.rest_3_) | copy-start | bytes 2359300
  91.5 12.0 %collective-permute-start.10 = (bf16[4,2,64,768]{3,2,1,0:T(8,128)(2,1)S(1)}, bf16[4,2,64,768]{3,2,1,0:T(8,128)(2,1)S(1)}, u32[]{:S(2)}, u32[]{:S(2)}) collective-permute-start(bf16[4,2,64,768]{3,2,1,0:T(8,128)(2,1)S(1)} %collective-permute-done.6.rest_3_), channel_id=1, source_target_pairs={{0,8},{8,0},{1,9},{9,1},{2,10},{10,2},{3,11},{11,3},{4,12},{12,4},... | collective-permute-start | bytes 2359304 | tf_op jit(solution)/shard_map/ppermute | solution.py:169
  97.1 9.1 %copy-start.3 = (bf16[4,2,64,768]{3,2,1,0:T(8,128)(2,1)}, bf16[4,2,64,768]{3,2,1,0:T(8,128)(2,1)S(1)}, u32[]{:S(2)}) copy-start(bf16[4,2,64,768]{3,2,1,0:T(8,128)(2,1)S(1)} %collective-permute-done.4.rest_1_) | copy-start | bytes 2359300
  97.1 6.5 %collective-permute-start.8 = (bf16[4,2,64,768]{3,2,1,0:T(8,128)(2,1)S(1)}, bf16[4,2,64,768]{3,2,1,0:T(8,128)(2,1)S(1)}, u32[]{:S(2)}, u32[]{:S(2)}) collective-permute-start(bf16[4,2,64,768]{3,2,1,0:T(8,128)(2,1)S(1)} %collective-permute-done.4.rest_1_), channel_id=1, source_target_pairs={{0,8},{8,0},{1,9},{9,1},{2,10},{10,2},{3,11},{11,3},{4,12},{12,4},... | collective-permute-start | bytes 2359304 | tf_op jit(solution)/shard_map/ppermute | solution.py:169
  99.0 7.2 %copy-start.4 = (bf16[4,2,64,768]{3,2,1,0:T(8,128)(2,1)}, bf16[4,2,64,768]{3,2,1,0:T(8,128)(2,1)S(1)}, u32[]{:S(2)}) copy-start(bf16[4,2,64,768]{3,2,1,0:T(8,128)(2,1)S(1)} %collective-permute-done.5.rest_2_) | copy-start | bytes 2359300
  99.0 6.6 %collective-permute-start.9 = (bf16[4,2,64,768]{3,2,1,0:T(8,128)(2,1)S(1)}, bf16[4,2,64,768]{3,2,1,0:T(8,128)(2,1)}, u32[]{:S(2)}, u32[]{:S(2)}) collective-permute-start(bf16[4,2,64,768]{3,2,1,0:T(8,128)(2,1)S(1)} %collective-permute-done.5.rest_2_), channel_id=1, source_target_pairs={{0,8},{8,0},{1,9},{9,1},{2,10},{10,2},{3,11},{11,3},{4,12},{12,4},... | collective-permute-start | bytes 2359304 | tf_op jit(solution)/shard_map/ppermute | solution.py:169
  103.5 0.9 copy-start.5
  103.5 1.1 copy-start.6
  104.7 0.9 copy-start.7
  111.0 11.4 %collective-permute-start.11 = (bf16[264,256]{1,0:T(8,128)(2,1)}, bf16[264,256]{1,0:T(8,128)(2,1)S(1)}, u32[]{:S(2)}, u32[]{:S(2)}) collective-permute-start(bf16[264,256]{1,0:T(8,128)(2,1)} %get-tuple-element.10), channel_id=1, source_target_pairs={{0,64},{64,128},{128,192},{192,256},{256,320},{320,384},{384,448},... | collective-permute-start | bytes 405512 | tf_op jit(solution)/shard_map/ppermute | solution.py:210
  112.3 10.1 %collective-permute-start.12 = (bf16[264,256]{1,0:T(8,128)(2,1)}, bf16[264,256]{1,0:T(8,128)(2,1)S(1)}, u32[]{:S(2)}, u32[]{:S(2)}) collective-permute-start(bf16[264,256]{1,0:T(8,128)(2,1)} %get-tuple-element.10), channel_id=1, source_target_pairs={{0,128},{64,192},{128,256},{192,320},{256,384},{320,448},{1,129},{... | collective-permute-start | bytes 405512 | tf_op jit(solution)/shard_map/ppermute | solution.py:211
  116.2 6.1 %copy-start.8 = (bf16[264,256]{1,0:T(8,128)(2,1)S(1)}, bf16[264,256]{1,0:T(8,128)(2,1)}, u32[]{:S(2)}) copy-start(bf16[264,256]{1,0:T(8,128)(2,1)} %get-tuple-element.10) | copy-start | bytes 405508
  122.5 11.2 %collective-permute-start.13 = (bf16[2,264,256]{2,1,0:T(8,128)(2,1)S(1)}, bf16[2,264,256]{2,1,0:T(8,128)(2,1)S(1)}, u32[]{:S(2)}, u32[]{:S(2)}) collective-permute-start(bf16[2,264,256]{2,1,0:T(8,128)(2,1)S(1)} %get-tuple-element.22), channel_id=1, source_target_pairs={{0,16},{16,32},{32,48},{48,0},{1,17},{17,33},{33,49},{49,1},{2,18}... | collective-permute-start | bytes 811016 | tf_op jit(solution)/shard_map/ppermute | solution.py:216
  124.4 12.8 %collective-permute-start.14 = (bf16[2,264,256]{2,1,0:T(8,128)(2,1)S(1)}, bf16[2,264,256]{2,1,0:T(8,128)(2,1)S(1)}, u32[]{:S(2)}, u32[]{:S(2)}) collective-permute-start(bf16[2,264,256]{2,1,0:T(8,128)(2,1)S(1)} %get-tuple-element.21), channel_id=1, source_target_pairs={{0,32},{16,48},{32,0},{48,16},{1,33},{17,49},{33,1},{49,17},{2,34}... | collective-permute-start | bytes 811016 | tf_op jit(solution)/shard_map/ppermute | solution.py:216
  126.3 19.1 %collective-permute-start.15 = (bf16[2,264,256]{2,1,0:T(8,128)(2,1)S(1)}, bf16[2,264,256]{2,1,0:T(8,128)(2,1)S(1)}, u32[]{:S(2)}, u32[]{:S(2)}) collective-permute-start(bf16[2,264,256]{2,1,0:T(8,128)(2,1)S(1)} %get-tuple-element.20), channel_id=1, source_target_pairs={{0,48},{16,0},{32,16},{48,32},{1,49},{17,1},{33,17},{49,33},{2,50}... | collective-permute-start | bytes 811016 | tf_op jit(solution)/shard_map/ppermute | solution.py:216
  145.6 4.8 %collective-permute-start.16 = (bf16[8,264,256]{2,1,0:T(8,128)(2,1)S(1)}, bf16[8,264,256]{2,1,0:T(8,128)(2,1)S(1)}, u32[]{:S(2)}, u32[]{:S(2)}) collective-permute-start(bf16[8,264,256]{2,1,0:T(8,128)(2,1)S(1)} %bitcast_dynamic-update-slice_fusion), channel_id=1, source_target_pairs={{0,8},{8,0},{1,9},{9,1},{2,10},{10,2},{3,11},{11,3},{4,12},{12,4},... | collective-permute-start | bytes 3244040 | tf_op jit(solution)/shard_map/ppermute | solution.py:218
  148.5 1.9 copy-start.1
  150.4 1.0 copy-start.9
Sparse Core Ops, SparseCore 0:
  9.4 81.8 all-gather.5
  94.5 64.0 all-gather.3
  164.6 97.9 reduce-scatter.1
where the time goes:
time: 270 us; the launch traced here: 269 us
  waiting for transfers between devices  149 us (55%)
  starting transfers between devices  72.2 us (27%)
  Pallas kernels  24 us (9%)
  between operations  13.5 us (5%)
  other arithmetic  5.56 us (2%)
  local copies, waits for them, and re-layouts  5.34 us (2%)
    reduce_scatter x1, waiting for transfers between devices, local(): lax.psum_scatter(partial_terms.reshape(n_tp * rows, cols), 'tp', scatter_...  98.1 us
    ppermute x1, starting transfers between devices, local(): o_away = lax.ppermute(o_block, 'zh', swap)  15.7 us
    ppermute x3, waiting for transfers between devices, local(): mine.append(lax.ppermute(two, 'x', ring(4, step)))  15.1 us
    ppermute x3, waiting for transfers between devices, local(): lax.ppermute(near, PLANE, plane_route(e, False))  13.6 us
    ppermute x1, starting transfers between devices, local(): away = lax.ppermute(weight, 'zh', swap)  13 us
    ppermute x3, starting transfers between devices, local(): lax.ppermute(near, PLANE, plane_route(e, False))  11 us
    ppermute x3, starting transfers between devices, local(): lax.ppermute(pair, PLANE, plane_route(d, True))  9.16 us
    pallas_call x1, Pallas kernels, local(): pl.pallas_call(attention_kernel, out_shape=jax.ShapeDtypeStruct((rows, q_...  9.05 us
  transfers between devices with their start and end apart: 21, of which 11 were waited for; matrix products, arithmetic and copies ran while one was open for 2% of the time, Pallas kernels for 7%

commit v1 on v0

--- a/solution.py
+++ b/solution.py
@@ -8,6 +8,7 @@
 
 HEAD = 128
 PLANE = ("y", "x", "core")
+FOLDED = [0, 2, 4, 6, 7, 5, 3, 1]
 
 
 def line(size, step):
@@ -75,7 +76,8 @@
     for j in range(n_tp):
         block = x_ref[j, :rows].astype(jnp.float32)
         gain = x_ref[j, pl.ds(rows, 1)].astype(jnp.float32)
-        normed_ref[:, j * cols : (j + 1) * cols] = (block * scale * gain).astype(jnp.bfloat16)
+        at = FOLDED[j] * cols
+        normed_ref[:, at : at + cols] = (block * scale * gain).astype(jnp.bfloat16)
     for copy in copies:
         copy.wait()
     out = jnp.dot(normed_ref[...], buffer[...], preferred_element_type=jnp.float32)
@@ -135,10 +137,10 @@
 
 
 def out_kernel(zh, a_ref, o_ref, out_ref):
-    del zh
-    for j in range(o_ref.shape[0]):
-        out_ref[j] = lax.dot_general(
-            a_ref[...], o_ref[j], (((1,), (1,)), ((), ())), preferred_element_type=jnp.float32
+    for n in range(o_ref.shape[0]):
+        block = (jnp.where(pl.program_id(0) == 0, n, 3 - n) + 2 * zh[0]) % 4
+        out_ref[n] = lax.dot_general(
+            a_ref[...], o_ref[block, 0], (((1,), (1,)), ((), ())), preferred_element_type=jnp.float32
         ).astype(jnp.bfloat16)
 
 
@@ -154,7 +156,7 @@
     swap = [(0, 1), (1, 0)]
 
     block = jnp.concatenate([tokens, jnp.broadcast_to(norm_gain[None], (8, cols))], axis=0)
-    whole = lax.all_gather(block, "tp", axis=0, tiled=False)
+    whole = lax.all_gather(block, "tp", axis=0, tiled=False, axis_index_groups=[FOLDED])
 
     weight = jnp.concatenate([q_weight, k_weight, v_weight], axis=1)
     away = lax.ppermute(weight, "zh", swap)
@@ -176,6 +178,7 @@
     cos_part, sin_part = jnp.cos(angles), jnp.sin(angles)
     cos_part = jnp.concatenate([cos_part, cos_part], axis=1)
     sin_part = jnp.concatenate([-sin_part, sin_part], axis=1)
+    doc_ids, pieces[4] = lax.optimization_barrier((doc_ids, pieces[4]))
     docs = doc_ids.astype(jnp.float32) + 1.0
     docs_rows = jnp.broadcast_to(docs[None].astype(jnp.bfloat16), (8, rows))
 
@@ -235,14 +238,18 @@
             grid=(2,),
             in_specs=[
                 pl.BlockSpec((rows, q_cols), lambda i, zh: (0, 0)),
-                pl.BlockSpec((half, cols, q_cols), lambda i, zh: ((i + zh[0]) % 2, 0, 0)),
+                pl.BlockSpec((half, 1, cols, q_cols), lambda i, zh: (0, i, 0, 0)),
             ],
             out_specs=pl.BlockSpec((half, rows, cols), lambda i, zh: (i, 0, 0)),
         ),
         name="out_projection",
-    )(where[:1], attended, o_rows)
+    )(where[:1], attended, o_rows.reshape(half, 2, cols, q_cols))
     return lax.psum_scatter(
-        partial_terms.reshape(n_tp * rows, cols), "tp", scatter_dimension=0, tiled=True
+        partial_terms.reshape(n_tp * rows, cols),
+        "tp",
+        scatter_dimension=0,
+        tiled=True,
+        axis_index_groups=[FOLDED],
     )
 
 

time: 270 us -> 255 us (0.944)
  waiting for transfers between devices: 149 us -> 134 us
    reduce_scatter x1, waiting for transfers between devices: 98.1 us -> 81.8 us  [local(): lax.psum_scatter(partial_terms.reshape(n_tp * rows, cols), 'tp', scatter_...]
  transfers between devices with their start and end apart: 21 -> 21, of which waited for: 11 -> 11; matrix products, arithmetic and copies ran while one was open for 2% -> 2% of each run, Pallas kernels for 7% -> 8%
where the time goes in v1:
time: 255 us; the launch traced here: 254 us
  waiting for transfers between devices  134 us (53%)
  starting transfers between devices  72.3 us (28%)
  Pallas kernels  23.9 us (9%)
  between operations  13.5 us (5%)
  other arithmetic  5.54 us (2%)
  local copies, waits for them, and re-layouts  5.12 us (2%)
    reduce_scatter x1, waiting for transfers between devices, local(): lax.psum_scatter(partial_terms.reshape(n_tp * rows, cols), 'tp', scatter_...  81.8 us
    ppermute x3, waiting for transfers between devices, local(): mine.append(lax.ppermute(two, 'x', ring(4, step)))  17.3 us
    ppermute x1, starting transfers between devices, local(): o_away = lax.ppermute(o_block, 'zh', swap)  15.7 us
    ppermute x3, waiting for transfers between devices, local(): lax.ppermute(near, PLANE, plane_route(e, False))  13.6 us
    ppermute x1, starting transfers between devices, local(): away = lax.ppermute(weight, 'zh', swap)  13 us
    ppermute x3, starting transfers between devices, local(): lax.ppermute(near, PLANE, plane_route(e, False))  10.9 us
    ppermute x3, starting transfers between devices, local(): lax.ppermute(pair, PLANE, plane_route(d, True))  9.16 us
    ppermute x3, waiting for transfers between devices, local(): lax.ppermute(pair, PLANE, plane_route(d, True))  9.05 us
  transfers between devices with their start and end apart: 21, of which 11 were waited for; matrix products, arithmetic and copies ran while one was open for 2% of the time, Pallas kernels for 8%

profile of v1, /device:TPU:6, one launch (start us, length us, event | category | flops | bytes accessed | tf_op | source)
XLA Modules:
  0.0 254.1 jit_solution(10720144038843931288)
XLA Ops:
  6.5 0.7 broadcast_in_dim.6
  7.3 1.7 pad_maximum_fusion.4
  9.0 0.0 all-gather.4.cloned.1.call-start
  9.0 15.7 %collective-permute-start.17 = (bf16[64,512]{1,0:T(8,128)(2,1)}, bf16[64,512]{1,0:T(8,128)(2,1)S(1)}, u32[]{:S(2)}, u32[]{:S(2)}) collective-permute-start(bf16[64,512]{1,0:T(8,128)(2,1)} %bitcast.41), channel_id=1, source_target_pairs={{0,256},{256,0},{1,257},{257,1},{2,258},{258,2},{3,259},{259,3},{4... | collective-permute-start | bytes 196616 | tf_op jit(solution)/shard_map/ppermute | solution.py:169
  24.7 4.5 %collective-permute-done.17 = bf16[64,512]{1,0:T(8,128)(2,1)S(1)} collective-permute-done((bf16[64,512]{1,0:T(8,128)(2,1)}, bf16[64,512]{1,0:T(8,128)(2,1)S(1)}, u32[]{:S(2)}, u32[]{:S(2)}) %collective-permute-start.17) | collective-permute-done | bytes 65568 | tf_op jit(solution)/shard_map/ppermute | solution.py:169
  29.3 1.5 pad_maximum_fusion.8
  30.9 13.0 %collective-permute-start = (bf16[64,768]{1,0:T(8,128)(2,1)S(1)}, bf16[64,768]{1,0:T(8,128)(2,1)S(1)}, u32[]{:S(2)}, u32[]{:S(2)}) collective-permute-start(bf16[64,768]{1,0:T(8,128)(2,1)S(1)} %constant_dynamic-update-slice_fusion), channel_id=1, source_target_pairs={{0,256},{256,0},{1,257},{257,1},{2,258},{258,2},{3,259},{259,3},{4... | collective-permute-start | bytes 294920 | tf_op jit(solution)/shard_map/ppermute | solution.py:162
  43.9 5.6 %collective-permute-done = bf16[64,768]{1,0:T(8,128)(2,1)S(1)} collective-permute-done((bf16[64,768]{1,0:T(8,128)(2,1)S(1)}, bf16[64,768]{1,0:T(8,128)(2,1)S(1)}, u32[]{:S(2)}, u32[]{:S(2)}) %collective-permute-start) | collective-permute-done | bytes 98336 | tf_op jit(solution)/shard_map/ppermute | solution.py:162
  49.6 2.7 %collective-permute-start.3 = (bf16[2,64,768]{2,1,0:T(8,128)(2,1)S(1)}, bf16[2,64,768]{2,1,0:T(8,128)(2,1)S(1)}, u32[]{:S(2)}, u32[]{:S(2)}) collective-permute-start(bf16[2,64,768]{2,1,0:T(8,128)(2,1)S(1)} %get-tuple-element.23), channel_id=1, source_target_pairs={{0,48},{8,200},{16,0},{24,216},{32,16},{40,232},{48,32},{56,248},{... | collective-permute-start | bytes 589832 | tf_op jit(solution)/shard_map/ppermute | solution.py:164
  52.3 4.3 %collective-permute-start.1 = (bf16[2,64,768]{2,1,0:T(8,128)(2,1)S(1)}, bf16[2,64,768]{2,1,0:T(8,128)(2,1)S(1)}, u32[]{:S(2)}, u32[]{:S(2)}) collective-permute-start(bf16[2,64,768]{2,1,0:T(8,128)(2,1)S(1)} %get-tuple-element.23), channel_id=1, source_target_pairs={{0,16},{8,72},{16,32},{24,88},{32,48},{40,104},{48,0},{56,120},{64... | collective-permute-start | bytes 589832 | tf_op jit(solution)/shard_map/ppermute | solution.py:164
  56.6 2.1 collective-permute-start.2
  58.8 1.1 collective-permute-done.1
  59.9 7.9 %collective-permute-done.2 = bf16[2,64,768]{2,1,0:T(8,128)(2,1)S(1)} collective-permute-done((bf16[2,64,768]{2,1,0:T(8,128)(2,1)S(1)}, bf16[2,64,768]{2,1,0:T(8,128)(2,1)S(1)}, u32[]{:S(2)}, u32[]{:S(2)}) %collective-permute-start.2) | collective-permute-done | bytes 196640 | tf_op jit(solution)/shard_map/ppermute | solution.py:164
  67.8 0.1 pad_maximum_fusion.rest_0_
  67.9 4.9 %collective-permute-start.7 = (bf16[4,2,64,768]{3,2,1,0:T(8,128)(2,1)S(1)}, bf16[4,2,64,768]{3,2,1,0:T(8,128)(2,1)S(1)}, u32[]{:S(2)}, u32[]{:S(2)}) collective-permute-start(bf16[4,2,64,768]{3,2,1,0:T(8,128)(2,1)S(1)} %pad_maximum_fusion.rest_0_), channel_id=1, source_target_pairs={{0,192},{8,56},{16,208},{24,8},{32,224},{40,24},{48,240},{56,40},{... | collective-permute-start | bytes 2359304 | tf_op jit(solution)/shard_map/ppermute | solution.py:166
  72.8 1.9 collective-permute-start.5
  74.8 4.1 %collective-permute-start.6 = (bf16[4,2,64,768]{3,2,1,0:T(8,128)(2,1)S(1)}, bf16[4,2,64,768]{3,2,1,0:T(8,128)(2,1)S(1)}, u32[]{:S(2)}, u32[]{:S(2)}) collective-permute-start(bf16[4,2,64,768]{3,2,1,0:T(8,128)(2,1)S(1)} %pad_maximum_fusion.rest_0_), channel_id=1, source_target_pairs={{0,128},{8,40},{16,144},{24,56},{32,160},{40,8},{48,176},{56,24},{... | collective-permute-start | bytes 2359304 | tf_op jit(solution)/shard_map/ppermute | solution.py:166
  78.8 1.9 collective-permute-start.4
  80.8 10.0 %collective-permute-done.7.rest_3_ = bf16[4,2,64,768]{3,2,1,0:T(8,128)(2,1)S(1)} collective-permute-done((bf16[4,2,64,768]{3,2,1,0:T(8,128)(2,1)S(1)}, bf16[4,2,64,768]{3,2,1,0:T(8,128)(2,1)S(1)}, u32[]{:S(2)}, u32[]{:S(2)}) %collective-permute-start.7) | collective-permute-done | bytes 786464 | tf_op jit(solution)/shard_map/ppermute | solution.py:166
  90.8 1.9 collective-permute-start.10
  92.7 3.7 %collective-permute-done.5.rest_1_ = bf16[4,2,64,768]{3,2,1,0:T(8,128)(2,1)S(1)} collective-permute-done((bf16[4,2,64,768]{3,2,1,0:T(8,128)(2,1)S(1)}, bf16[4,2,64,768]{3,2,1,0:T(8,128)(2,1)S(1)}, u32[]{:S(2)}, u32[]{:S(2)}) %collective-permute-start.5) | collective-permute-done | bytes 786464 | tf_op jit(solution)/shard_map/ppermute | solution.py:166
  96.4 1.9 collective-permute-start.8
  98.3 2.4 collective-permute-start.9
  100.7 0.7 pad_add_fusion.where
  101.4 0.5 fusion
  101.9 0.9 pad_maximum_fusion.6
  102.8 0.9 copy-done.5
  103.7 0.9 copy-done.6
  104.6 0.6 broadcast_in_dim.7.docs_ref
  105.2 4.7 %kv_projection.1 = (bf16[264,256]{1,0:T(8,128)(2,1)}, bf16[256,4096]{1,0:T(8,128)(2,1)}) custom-call(s32[4]{0:T(128)} %pad_add_fusion.where, bf16[8,264,512]{2,1,0:T(8,128)(2,1)} %bitcast.34, bf16[8,256]{1,0:T(8,128)(2,1)} %broadcast_in_dim.7.docs_ref, f32[256,128]{1,0:T(8,128)} %get-tuple-element.32.cos_ref, f32[256,128]{1,0:T(8,128)} %get-tuple-element.33.sin_ref, ...), custom_call_target="tpu_custom_call" | custom-call | tf_op jit(solution)/shard_map/kv_projection/pallas_call | solution.py:186
  109.9 1.3 collective-permute-start.11
  111.2 4.1 %collective-permute-start.12 = (bf16[264,256]{1,0:T(8,128)(2,1)}, bf16[264,256]{1,0:T(8,128)(2,1)S(1)}, u32[]{:S(2)}, u32[]{:S(2)}) collective-permute-start(bf16[264,256]{1,0:T(8,128)(2,1)} %get-tuple-element.14), channel_id=1, source_target_pairs={{0,128},{64,192},{128,256},{192,320},{256,384},{320,448},{1,129},{... | collective-permute-start | bytes 405512 | tf_op jit(solution)/shard_map/ppermute | solution.py:214
  115.3 6.1 %q_projection.1.q_ref = bf16[4,256,128]{2,1,0:T(8,128)(2,1)} custom-call(s32[4]{0:T(128)} %pad_add_fusion.where, bf16[256,4096]{1,0:T(8,128)(2,1)} %get-tuple-element.15.normed_ref, f32[256,128]{1,0:T(8,128)} %get-tuple-element.32.cos_ref, f32[256,128]{1,0:T(8,128)} %get-tuple-element.33.sin_ref, bf16[4,2,64,768]{3,2,1,0:T(8,128)(2,1)} %copy-done, ...), custom_call_target="tpu_custom_call" | custom-call | flops 1073741824 | bytes 6291456 | tf_op jit(solution)/shard_map/q_projection/pallas_call | solution.py:199
  121.5 0.1 pad_maximum_fusion.1
  121.6 1.9 collective-permute-start.13
  123.5 1.9 collective-permute-start.14
  125.4 3.9 %collective-permute-start.15 = (bf16[2,264,256]{2,1,0:T(8,128)(2,1)S(1)}, bf16[2,264,256]{2,1,0:T(8,128)(2,1)S(1)}, u32[]{:S(2)}, u32[]{:S(2)}) collective-permute-start(bf16[2,264,256]{2,1,0:T(8,128)(2,1)S(1)} %get-tuple-element.24), channel_id=1, source_target_pairs={{0,48},{16,0},{32,16},{48,32},{1,49},{17,1},{33,17},{49,33},{2,50}... | collective-permute-start | bytes 811016 | tf_op jit(solution)/shard_map/ppermute | solution.py:219
  129.4 3.5 %collective-permute-done.13 = bf16[2,264,256]{2,1,0:T(8,128)(2,1)S(1)} collective-permute-done((bf16[2,264,256]{2,1,0:T(8,128)(2,1)S(1)}, bf16[2,264,256]{2,1,0:T(8,128)(2,1)S(1)}, u32[]{:S(2)}, u32[]{:S(2)}) %collective-permute-start.13) | collective-permute-done | bytes 270368 | tf_op jit(solution)/shard_map/ppermute | solution.py:219
  132.8 5.8 %collective-permute-done.14 = bf16[2,264,256]{2,1,0:T(8,128)(2,1)S(1)} collective-permute-done((bf16[2,264,256]{2,1,0:T(8,128)(2,1)S(1)}, bf16[2,264,256]{2,1,0:T(8,128)(2,1)S(1)}, u32[]{:S(2)}, u32[]{:S(2)}) %collective-permute-start.14) | collective-permute-done | bytes 270368 | tf_op jit(solution)/shard_map/ppermute | solution.py:219
  138.7 8.0 %collective-permute-done.15 = bf16[2,264,256]{2,1,0:T(8,128)(2,1)S(1)} collective-permute-done((bf16[2,264,256]{2,1,0:T(8,128)(2,1)S(1)}, bf16[2,264,256]{2,1,0:T(8,128)(2,1)S(1)}, u32[]{:S(2)}, u32[]{:S(2)}) %collective-permute-start.15) | collective-permute-done | bytes 270368 | tf_op jit(solution)/shard_map/ppermute | solution.py:219
  146.8 0.1 copy.15
  146.9 2.2 collective-permute-start.16
  149.1 0.8 copy.8.docs_ref
  149.9 1.6 collective-permute-done.16.other_ref
  151.5 1.0 copy-done.8
  152.5 9.0 %attention.1.a_ref = bf16[256,512]{1,0:T(8,128)(2,1)} custom-call(bf16[4,256,128]{2,1,0:T(8,128)(2,1)} %q_projection.1.q_ref, f32[256,1]{1,0:T(8,128)} %copy.8.docs_ref, bf16[8,264,256]{2,1,0:T(8,128)(2,1)} %copy-done.1, bf16[8,264,256]{2,1,0:T(8,128)(2,1)} %copy-done.8), custom_call_target="tpu_custom_call" | custom-call | tf_op jit(solution)/shard_map/attention/pallas_call | solution.py:224
  161.6 4.1 %out_projection.1 = bf16[8,256,512]{2,1,0:T(8,128)(2,1)} custom-call(s32[1]{0:T(128)} %bitcast.zh, bf16[256,512]{1,0:T(8,128)(2,1)} %attention.1.a_ref, bf16[4,2,512,512]{3,2,1,0:T(8,128)(2,1)} %bitcast.33), custom_call_target="tpu_custom_call" | custom-call | tf_op jit(solution)/shard_map/out_projection/pallas_call | solution.py:233
  165.7 81.8 %reduce-scatter.2.cloned.1.call-done = bf16[256,512]{1,0:T(8,128)(2,1)} async-done(((bf16[2048,512]{1,0:T(8,128)(2,1)}), bf16[256,512]{1,0:T(8,128)(2,1)}) %reduce-scatter.2.cloned.1.call-update) | async-done | bytes 262160 | tf_op jit(solution)/shard_map/reduce_scatter | solution.py:247
  (52 shorter events, 0.4 us)
Async XLA Ops:
  6.5 24.3 %copy-start.9 = (bf16[64,512]{1,0:T(8,128)(2,1)S(1)}, bf16[64,512]{1,0:T(8,128)(2,1)}, u32[]{:S(2)}) copy-start(bf16[64,512]{1,0:T(8,128)(2,1)} %param.10) | copy-start | bytes 196612
  6.5 24.3 %copy-start.10 = (bf16[64,128]{1,0:T(8,128)(2,1)S(1)}, bf16[64,128]{1,0:T(8,128)(2,1)}, u32[]{:S(2)}) copy-start(bf16[64,128]{1,0:T(8,128)(2,1)} %param.11) | copy-start | bytes 49156
  6.5 24.4 %copy-start.11 = (bf16[64,128]{1,0:T(8,128)(2,1)S(1)}, bf16[64,128]{1,0:T(8,128)(2,1)}, u32[]{:S(2)}) copy-start(bf16[64,128]{1,0:T(8,128)(2,1)} %param.12) | copy-start | bytes 49156
  6.5 98.1 %all-gather.6.cloned.1.call-start = ((), (), s32[]{:S(2)}) async-start(), calls=%async_computation.3 | async-start | bytes 2433024 | tf_op jit(solution)/shard_map/all_gather | solution.py:159
  9.0 152.6 %all-gather.4.cloned.1.call-start = ((), (), s32[]{:S(2)}) async-start(), calls=%async_computation.1 | async-start | bytes 4325376 | tf_op jit(solution)/shard_map/all_gather | solution.py:172
  9.0 20.3 %collective-permute-start.17 = (bf16[64,512]{1,0:T(8,128)(2,1)}, bf16[64,512]{1,0:T(8,128)(2,1)S(1)}, u32[]{:S(2)}, u32[]{:S(2)}) collective-permute-start(bf16[64,512]{1,0:T(8,128)(2,1)} %bitcast.41), channel_id=1, source_target_pairs={{0,256},{256,0},{1,257},{257,1},{2,258},{258,2},{3,259},{259,3},{4... | collective-permute-start | bytes 196616 | tf_op jit(solution)/shard_map/ppermute | solution.py:169
  30.8 216.7 %reduce-scatter.2.cloned.1.call-start = ((), (), s32[]{:S(2)}) async-start(), calls=%async_computation.2 | async-start | bytes 2359296 | tf_op jit(solution)/shard_map/reduce_scatter | solution.py:247
  30.9 18.6 %collective-permute-start = (bf16[64,768]{1,0:T(8,128)(2,1)S(1)}, bf16[64,768]{1,0:T(8,128)(2,1)S(1)}, u32[]{:S(2)}, u32[]{:S(2)}) collective-permute-start(bf16[64,768]{1,0:T(8,128)(2,1)S(1)} %constant_dynamic-update-slice_fusion), channel_id=1, source_target_pairs={{0,256},{256,0},{1,257},{257,1},{2,258},{258,2},{3,259},{259,3},{4... | collective-permute-start | bytes 294920 | tf_op jit(solution)/shard_map/ppermute | solution.py:162
  49.6 9.2 %collective-permute-start.3 = (bf16[2,64,768]{2,1,0:T(8,128)(2,1)S(1)}, bf16[2,64,768]{2,1,0:T(8,128)(2,1)S(1)}, u32[]{:S(2)}, u32[]{:S(2)}) collective-permute-start(bf16[2,64,768]{2,1,0:T(8,128)(2,1)S(1)} %get-tuple-element.23), channel_id=1, source_target_pairs={{0,48},{8,200},{16,0},{24,216},{32,16},{40,232},{48,32},{56,248},{... | collective-permute-start | bytes 589832 | tf_op jit(solution)/shard_map/ppermute | solution.py:164
  52.3 7.6 %collective-permute-start.1 = (bf16[2,64,768]{2,1,0:T(8,128)(2,1)S(1)}, bf16[2,64,768]{2,1,0:T(8,128)(2,1)S(1)}, u32[]{:S(2)}, u32[]{:S(2)}) collective-permute-start(bf16[2,64,768]{2,1,0:T(8,128)(2,1)S(1)} %get-tuple-element.23), channel_id=1, source_target_pairs={{0,16},{8,72},{16,32},{24,88},{32,48},{40,104},{48,0},{56,120},{64... | collective-permute-start | bytes 589832 | tf_op jit(solution)/shard_map/ppermute | solution.py:164
  56.6 11.2 %collective-permute-start.2 = (bf16[2,64,768]{2,1,0:T(8,128)(2,1)S(1)}, bf16[2,64,768]{2,1,0:T(8,128)(2,1)S(1)}, u32[]{:S(2)}, u32[]{:S(2)}) collective-permute-start(bf16[2,64,768]{2,1,0:T(8,128)(2,1)S(1)} %get-tuple-element.23), channel_id=1, source_target_pairs={{0,32},{8,136},{16,48},{24,152},{32,0},{40,168},{48,16},{56,184},{... | collective-permute-start | bytes 589832 | tf_op jit(solution)/shard_map/ppermute | solution.py:164
  67.8 35.0 %copy-start.12 = (s32[256]{0:T(256)S(1)}, s32[256]{0:T(256)}, u32[]{:S(2)}) copy-start(s32[256]{0:T(256)} %param.9) | copy-start | bytes 3076
  67.9 37.3 %copy-start = (bf16[4,2,64,768]{3,2,1,0:T(8,128)(2,1)}, bf16[4,2,64,768]{3,2,1,0:T(8,128)(2,1)S(1)}, u32[]{:S(2)}) copy-start(bf16[4,2,64,768]{3,2,1,0:T(8,128)(2,1)S(1)} %pad_maximum_fusion.rest_0_) | copy-start | bytes 2359300
  67.9 22.9 %collective-permute-start.7 = (bf16[4,2,64,768]{3,2,1,0:T(8,128)(2,1)S(1)}, bf16[4,2,64,768]{3,2,1,0:T(8,128)(2,1)S(1)}, u32[]{:S(2)}, u32[]{:S(2)}) collective-permute-start(bf16[4,2,64,768]{3,2,1,0:T(8,128)(2,1)S(1)} %pad_maximum_fusion.rest_0_), channel_id=1, source_target_pairs={{0,192},{8,56},{16,208},{24,8},{32,224},{40,24},{48,240},{56,40},{... | collective-permute-start | bytes 2359304 | tf_op jit(solution)/shard_map/ppermute | solution.py:166
  72.8 23.5 %collective-permute-start.5 = (bf16[4,2,64,768]{3,2,1,0:T(8,128)(2,1)S(1)}, bf16[4,2,64,768]{3,2,1,0:T(8,128)(2,1)S(1)}, u32[]{:S(2)}, u32[]{:S(2)}) collective-permute-start(bf16[4,2,64,768]{3,2,1,0:T(8,128)(2,1)S(1)} %pad_maximum_fusion.rest_0_), channel_id=1, source_target_pairs={{0,64},{8,24},{16,80},{24,40},{32,96},{40,56},{48,112},{56,8},{64,... | collective-permute-start | bytes 2359304 | tf_op jit(solution)/shard_map/ppermute | solution.py:166
  74.8 23.5 %collective-permute-start.6 = (bf16[4,2,64,768]{3,2,1,0:T(8,128)(2,1)S(1)}, bf16[4,2,64,768]{3,2,1,0:T(8,128)(2,1)S(1)}, u32[]{:S(2)}, u32[]{:S(2)}) collective-permute-start(bf16[4,2,64,768]{3,2,1,0:T(8,128)(2,1)S(1)} %pad_maximum_fusion.rest_0_), channel_id=1, source_target_pairs={{0,128},{8,40},{16,144},{24,56},{32,160},{40,8},{48,176},{56,24},{... | collective-permute-start | bytes 2359304 | tf_op jit(solution)/shard_map/ppermute | solution.py:166
  78.8 23.9 %collective-permute-start.4 = (bf16[4,2,64,768]{3,2,1,0:T(8,128)(2,1)S(1)}, bf16[4,2,64,768]{3,2,1,0:T(8,128)(2,1)}, u32[]{:S(2)}, u32[]{:S(2)}) collective-permute-start(bf16[4,2,64,768]{3,2,1,0:T(8,128)(2,1)S(1)} %pad_maximum_fusion.rest_0_), channel_id=1, source_target_pairs={{0,8},{8,0},{1,9},{9,1},{2,10},{10,2},{3,11},{11,3},{4,12},{12,4},... | collective-permute-start | bytes 2359304 | tf_op jit(solution)/shard_map/ppermute | solution.py:171
  90.8 14.4 %copy-start.2 = (bf16[4,2,64,768]{3,2,1,0:T(8,128)(2,1)}, bf16[4,2,64,768]{3,2,1,0:T(8,128)(2,1)S(1)}, u32[]{:S(2)}) copy-start(bf16[4,2,64,768]{3,2,1,0:T(8,128)(2,1)S(1)} %collective-permute-done.7.rest_3_) | copy-start | bytes 2359300
  90.8 12.0 %collective-permute-start.10 = (bf16[4,2,64,768]{3,2,1,0:T(8,128)(2,1)S(1)}, bf16[4,2,64,768]{3,2,1,0:T(8,128)(2,1)S(1)}, u32[]{:S(2)}, u32[]{:S(2)}) collective-permute-start(bf16[4,2,64,768]{3,2,1,0:T(8,128)(2,1)S(1)} %collective-permute-done.7.rest_3_), channel_id=1, source_target_pairs={{0,8},{8,0},{1,9},{9,1},{2,10},{10,2},{3,11},{11,3},{4,12},{12,4},... | collective-permute-start | bytes 2359304 | tf_op jit(solution)/shard_map/ppermute | solution.py:171
  96.4 8.9 %copy-start.3 = (bf16[4,2,64,768]{3,2,1,0:T(8,128)(2,1)}, bf16[4,2,64,768]{3,2,1,0:T(8,128)(2,1)S(1)}, u32[]{:S(2)}) copy-start(bf16[4,2,64,768]{3,2,1,0:T(8,128)(2,1)S(1)} %collective-permute-done.5.rest_1_) | copy-start | bytes 2359300
  96.4 6.4 %collective-permute-start.8 = (bf16[4,2,64,768]{3,2,1,0:T(8,128)(2,1)S(1)}, bf16[4,2,64,768]{3,2,1,0:T(8,128)(2,1)S(1)}, u32[]{:S(2)}, u32[]{:S(2)}) collective-permute-start(bf16[4,2,64,768]{3,2,1,0:T(8,128)(2,1)S(1)} %collective-permute-done.5.rest_1_), channel_id=1, source_target_pairs={{0,8},{8,0},{1,9},{9,1},{2,10},{10,2},{3,11},{11,3},{4,12},{12,4},... | collective-permute-start | bytes 2359304 | tf_op jit(solution)/shard_map/ppermute | solution.py:171
  98.3 6.9 %copy-start.4 = (bf16[4,2,64,768]{3,2,1,0:T(8,128)(2,1)}, bf16[4,2,64,768]{3,2,1,0:T(8,128)(2,1)S(1)}, u32[]{:S(2)}) copy-start(bf16[4,2,64,768]{3,2,1,0:T(8,128)(2,1)S(1)} %collective-permute-done.6.rest_2_) | copy-start | bytes 2359300
  98.3 6.3 %collective-permute-start.9 = (bf16[4,2,64,768]{3,2,1,0:T(8,128)(2,1)S(1)}, bf16[4,2,64,768]{3,2,1,0:T(8,128)(2,1)}, u32[]{:S(2)}, u32[]{:S(2)}) collective-permute-start(bf16[4,2,64,768]{3,2,1,0:T(8,128)(2,1)S(1)} %collective-permute-done.6.rest_2_), channel_id=1, source_target_pairs={{0,8},{8,0},{1,9},{9,1},{2,10},{10,2},{3,11},{11,3},{4,12},{12,4},... | collective-permute-start | bytes 2359304 | tf_op jit(solution)/shard_map/ppermute | solution.py:171
  102.8 0.9 copy-start.5
  103.7 0.9 copy-start.6
  109.9 11.5 %collective-permute-start.11 = (bf16[264,256]{1,0:T(8,128)(2,1)}, bf16[264,256]{1,0:T(8,128)(2,1)S(1)}, u32[]{:S(2)}, u32[]{:S(2)}) collective-permute-start(bf16[264,256]{1,0:T(8,128)(2,1)} %get-tuple-element.14), channel_id=1, source_target_pairs={{0,64},{64,128},{128,192},{192,256},{256,320},{320,384},{384,448},... | collective-permute-start | bytes 405512 | tf_op jit(solution)/shard_map/ppermute | solution.py:213
  111.2 10.2 %collective-permute-start.12 = (bf16[264,256]{1,0:T(8,128)(2,1)}, bf16[264,256]{1,0:T(8,128)(2,1)S(1)}, u32[]{:S(2)}, u32[]{:S(2)}) collective-permute-start(bf16[264,256]{1,0:T(8,128)(2,1)} %get-tuple-element.14), channel_id=1, source_target_pairs={{0,128},{64,192},{128,256},{192,320},{256,384},{320,448},{1,129},{... | collective-permute-start | bytes 405512 | tf_op jit(solution)/shard_map/ppermute | solution.py:214
  115.3 6.1 %copy-start.7 = (bf16[264,256]{1,0:T(8,128)(2,1)S(1)}, bf16[264,256]{1,0:T(8,128)(2,1)}, u32[]{:S(2)}) copy-start(bf16[264,256]{1,0:T(8,128)(2,1)} %get-tuple-element.14) | copy-start | bytes 405508
  121.6 11.2 %collective-permute-start.13 = (bf16[2,264,256]{2,1,0:T(8,128)(2,1)S(1)}, bf16[2,264,256]{2,1,0:T(8,128)(2,1)S(1)}, u32[]{:S(2)}, u32[]{:S(2)}) collective-permute-start(bf16[2,264,256]{2,1,0:T(8,128)(2,1)S(1)} %get-tuple-element.26), channel_id=1, source_target_pairs={{0,16},{16,32},{32,48},{48,0},{1,17},{17,33},{33,49},{49,1},{2,18}... | collective-permute-start | bytes 811016 | tf_op jit(solution)/shard_map/ppermute | solution.py:219
  123.5 15.2 %collective-permute-start.14 = (bf16[2,264,256]{2,1,0:T(8,128)(2,1)S(1)}, bf16[2,264,256]{2,1,0:T(8,128)(2,1)S(1)}, u32[]{:S(2)}, u32[]{:S(2)}) collective-permute-start(bf16[2,264,256]{2,1,0:T(8,128)(2,1)S(1)} %get-tuple-element.25), channel_id=1, source_target_pairs={{0,32},{16,48},{32,0},{48,16},{1,33},{17,49},{33,1},{49,17},{2,34}... | collective-permute-start | bytes 811016 | tf_op jit(solution)/shard_map/ppermute | solution.py:219
  125.4 21.3 %collective-permute-start.15 = (bf16[2,264,256]{2,1,0:T(8,128)(2,1)S(1)}, bf16[2,264,256]{2,1,0:T(8,128)(2,1)S(1)}, u32[]{:S(2)}, u32[]{:S(2)}) collective-permute-start(bf16[2,264,256]{2,1,0:T(8,128)(2,1)S(1)} %get-tuple-element.24), channel_id=1, source_target_pairs={{0,48},{16,0},{32,16},{48,32},{1,49},{17,1},{33,17},{49,33},{2,50}... | collective-permute-start | bytes 811016 | tf_op jit(solution)/shard_map/ppermute | solution.py:219
  146.9 4.6 %collective-permute-start.16 = (bf16[8,264,256]{2,1,0:T(8,128)(2,1)S(1)}, bf16[8,264,256]{2,1,0:T(8,128)(2,1)S(1)}, u32[]{:S(2)}, u32[]{:S(2)}) collective-permute-start(bf16[8,264,256]{2,1,0:T(8,128)(2,1)S(1)} %bitcast_dynamic-update-slice_fusion), channel_id=1, source_target_pairs={{0,8},{8,0},{1,9},{9,1},{2,10},{10,2},{3,11},{11,3},{4,12},{12,4},... | collective-permute-start | bytes 3244040 | tf_op jit(solution)/shard_map/ppermute | solution.py:221
  149.9 1.6 copy-start.1
  151.5 1.0 copy-start.8
Sparse Core Ops, SparseCore 0:
  9.4 73.9 all-gather.5
  86.6 64.3 all-gather.3
  165.8 81.6 reduce-scatter.1

commit v2 on v1

--- a/solution.py
+++ b/solution.py
@@ -9,10 +9,6 @@
 HEAD = 128
 PLANE = ("y", "x", "core")
 FOLDED = [0, 2, 4, 6, 7, 5, 3, 1]
-
-
-def line(size, step):
-    return [(i, i + step) for i in range(size) if 0 <= i + step < size]
 
 
 def ring(size, step):
@@ -178,7 +174,6 @@
     cos_part, sin_part = jnp.cos(angles), jnp.sin(angles)
     cos_part = jnp.concatenate([cos_part, cos_part], axis=1)
     sin_part = jnp.concatenate([-sin_part, sin_part], axis=1)
-    doc_ids, pieces[4] = lax.optimization_barrier((doc_ids, pieces[4]))
     docs = doc_ids.astype(jnp.float32) + 1.0
     docs_rows = jnp.broadcast_to(docs[None].astype(jnp.bfloat16), (8, rows))
 
@@ -210,8 +205,14 @@
         name="q_projection",
     )(where, normed, cos_part, sin_part, *pieces)
 
-    back_1 = lax.ppermute(tile, ("zh", "y"), line(8, 1))
-    back_2 = lax.ppermute(tile, ("zh", "y"), line(8, 2))
+    crossed = lax.ppermute(tile, ("zh", "y"), [(2, 6), (3, 7)])
+    carried = (zh == 1) & (y >= 2)
+    sent = jnp.where(carried, crossed, tile)
+    back_2 = lax.ppermute(sent, ("zh", "y"), [(0, 2), (1, 3), (4, 6), (5, 7), (6, 4), (7, 5)])
+    sent = jnp.where(carried & (y == 3), crossed, tile)
+    back_1 = lax.ppermute(
+        sent, ("zh", "y"), [(0, 1), (1, 2), (2, 3), (4, 5), (5, 6), (6, 7), (7, 4)]
+    )
     back_1, back_2, q_rot = lax.optimization_barrier((back_1, back_2, q_rot))
     mine = []
     for step in range(1, 4):

time: 255 us -> 254 us (level)
  waiting for transfers between devices: 134 us -> 114 us
  starting transfers between devices: 72.3 us -> 90 us
    ppermute x2 -> x3, starting transfers between devices: 5.37 us -> 23.1 us  [the longest x1 21.2 us: local(): lax.ppermute(sent, ('zh', 'y'), [(0, 2), (1, 3), (4, 6), (5, 7), (6, 4),...]
    reduce_scatter x1, waiting for transfers between devices: 81.8 us -> 68.7 us  [local(): lax.psum_scatter(partial_terms.reshape(n_tp * rows, cols), 'tp', scatter_...]
    ppermute x3, waiting for transfers between devices: 17.3 us -> 10.8 us  [local(): mine.append(lax.ppermute(two, 'x', ring(4, step)))]
  transfers between devices with their start and end apart: 21 -> 22, of which waited for: 11 -> 11; matrix products, arithmetic and copies ran while one was open for 2% -> 2% of each run, Pallas kernels for 8% -> 8%
where the time goes in v2:
time: 254 us; the launch traced here: 253 us
  waiting for transfers between devices  114 us (45%)
  starting transfers between devices  90 us (35%)
  Pallas kernels  24 us (9%)
  between operations  13.6 us (5%)
  other arithmetic  6.39 us (3%)
  local copies, waits for them, and re-layouts  5.36 us (2%)
    reduce_scatter x1, waiting for transfers between devices, local(): lax.psum_scatter(partial_terms.reshape(n_tp * rows, cols), 'tp', scatter_...  68.7 us
    ppermute x1, starting transfers between devices, local(): lax.ppermute(sent, ('zh', 'y'), [(0, 2), (1, 3), (4, 6), (5, 7), (6, 4),...  21.2 us
    ppermute x1, starting transfers between devices, local(): o_away = lax.ppermute(o_block, 'zh', swap)  15.7 us
    ppermute x3, waiting for transfers between devices, local(): lax.ppermute(near, PLANE, plane_route(e, False))  13.6 us
    ppermute x1, starting transfers between devices, local(): away = lax.ppermute(weight, 'zh', swap)  13 us
    ppermute x3, starting transfers between devices, local(): lax.ppermute(near, PLANE, plane_route(e, False))  10.9 us
    ppermute x3, waiting for transfers between devices, local(): mine.append(lax.ppermute(two, 'x', ring(4, step)))  10.8 us
    ppermute x3, starting transfers between devices, local(): lax.ppermute(pair, PLANE, plane_route(d, True))  9.13 us
  transfers between devices with their start and end apart: 22, of which 11 were waited for; matrix products, arithmetic and copies ran while one was open for 2% of the time, Pallas kernels for 8%

profile of v2, /device:TPU:6, one launch (start us, length us, event | category | flops | bytes accessed | tf_op | source)
XLA Modules:
  0.0 253.3 jit_solution(16382941193224797516)
XLA Ops:
  6.5 0.7 broadcast_in_dim.6
  7.3 1.7 pad_maximum_fusion.4
  9.0 15.7 %collective-permute-start.18 = (bf16[64,512]{1,0:T(8,128)(2,1)}, bf16[64,512]{1,0:T(8,128)(2,1)S(1)}, u32[]{:S(2)}, u32[]{:S(2)}) collective-permute-start(bf16[64,512]{1,0:T(8,128)(2,1)} %bitcast.41), channel_id=1, source_target_pairs={{0,256},{256,0},{1,257},{257,1},{2,258},{258,2},{3,259},{259,3},{4... | collective-permute-start | bytes 196616 | tf_op jit(solution)/shard_map/ppermute | solution.py:165
  24.8 4.5 %collective-permute-done.18 = bf16[64,512]{1,0:T(8,128)(2,1)S(1)} collective-permute-done((bf16[64,512]{1,0:T(8,128)(2,1)}, bf16[64,512]{1,0:T(8,128)(2,1)S(1)}, u32[]{:S(2)}, u32[]{:S(2)}) %collective-permute-start.18) | collective-permute-done | bytes 65568 | tf_op jit(solution)/shard_map/ppermute | solution.py:165
  29.3 1.5 pad_maximum_fusion.8
  30.9 13.0 %collective-permute-start = (bf16[64,768]{1,0:T(8,128)(2,1)S(1)}, bf16[64,768]{1,0:T(8,128)(2,1)S(1)}, u32[]{:S(2)}, u32[]{:S(2)}) collective-permute-start(bf16[64,768]{1,0:T(8,128)(2,1)S(1)} %constant_dynamic-update-slice_fusion), channel_id=1, source_target_pairs={{0,256},{256,0},{1,257},{257,1},{2,258},{258,2},{3,259},{259,3},{4... | collective-permute-start | bytes 294920 | tf_op jit(solution)/shard_map/ppermute | solution.py:158
  43.9 5.6 %collective-permute-done = bf16[64,768]{1,0:T(8,128)(2,1)S(1)} collective-permute-done((bf16[64,768]{1,0:T(8,128)(2,1)S(1)}, bf16[64,768]{1,0:T(8,128)(2,1)S(1)}, u32[]{:S(2)}, u32[]{:S(2)}) %collective-permute-start) | collective-permute-done | bytes 98336 | tf_op jit(solution)/shard_map/ppermute | solution.py:158
  49.6 2.7 %collective-permute-start.3 = (bf16[2,64,768]{2,1,0:T(8,128)(2,1)S(1)}, bf16[2,64,768]{2,1,0:T(8,128)(2,1)S(1)}, u32[]{:S(2)}, u32[]{:S(2)}) collective-permute-start(bf16[2,64,768]{2,1,0:T(8,128)(2,1)S(1)} %get-tuple-element.21), channel_id=1, source_target_pairs={{0,48},{8,200},{16,0},{24,216},{32,16},{40,232},{48,32},{56,248},{... | collective-permute-start | bytes 589832 | tf_op jit(solution)/shard_map/ppermute | solution.py:160
  52.3 4.3 %collective-permute-start.1 = (bf16[2,64,768]{2,1,0:T(8,128)(2,1)S(1)}, bf16[2,64,768]{2,1,0:T(8,128)(2,1)S(1)}, u32[]{:S(2)}, u32[]{:S(2)}) collective-permute-start(bf16[2,64,768]{2,1,0:T(8,128)(2,1)S(1)} %get-tuple-element.21), channel_id=1, source_target_pairs={{0,16},{8,72},{16,32},{24,88},{32,48},{40,104},{48,0},{56,120},{64... | collective-permute-start | bytes 589832 | tf_op jit(solution)/shard_map/ppermute | solution.py:160
  56.6 2.1 collective-permute-start.2
  58.7 1.2 collective-permute-done.1
  59.9 7.9 %collective-permute-done.2 = bf16[2,64,768]{2,1,0:T(8,128)(2,1)S(1)} collective-permute-done((bf16[2,64,768]{2,1,0:T(8,128)(2,1)S(1)}, bf16[2,64,768]{2,1,0:T(8,128)(2,1)S(1)}, u32[]{:S(2)}, u32[]{:S(2)}) %collective-permute-start.2) | collective-permute-done | bytes 196640 | tf_op jit(solution)/shard_map/ppermute | solution.py:160
  67.8 0.1 pad_maximum_fusion.rest_0_
  67.9 4.9 %collective-permute-start.6 = (bf16[4,2,64,768]{3,2,1,0:T(8,128)(2,1)S(1)}, bf16[4,2,64,768]{3,2,1,0:T(8,128)(2,1)S(1)}, u32[]{:S(2)}, u32[]{:S(2)}) collective-permute-start(bf16[4,2,64,768]{3,2,1,0:T(8,128)(2,1)S(1)} %pad_maximum_fusion.rest_0_), channel_id=1, source_target_pairs={{0,192},{8,56},{16,208},{24,8},{32,224},{40,24},{48,240},{56,40},{... | collective-permute-start | bytes 2359304 | tf_op jit(solution)/shard_map/ppermute | solution.py:162
  72.8 1.9 collective-permute-start.4
  74.7 4.1 %collective-permute-start.5 = (bf16[4,2,64,768]{3,2,1,0:T(8,128)(2,1)S(1)}, bf16[4,2,64,768]{3,2,1,0:T(8,128)(2,1)S(1)}, u32[]{:S(2)}, u32[]{:S(2)}) collective-permute-start(bf16[4,2,64,768]{3,2,1,0:T(8,128)(2,1)S(1)} %pad_maximum_fusion.rest_0_), channel_id=1, source_target_pairs={{0,128},{8,40},{16,144},{24,56},{32,160},{40,8},{48,176},{56,24},{... | collective-permute-start | bytes 2359304 | tf_op jit(solution)/shard_map/ppermute | solution.py:162
  78.9 1.9 collective-permute-start.7
  80.8 9.9 %collective-permute-done.6.rest_3_ = bf16[4,2,64,768]{3,2,1,0:T(8,128)(2,1)S(1)} collective-permute-done((bf16[4,2,64,768]{3,2,1,0:T(8,128)(2,1)S(1)}, bf16[4,2,64,768]{3,2,1,0:T(8,128)(2,1)S(1)}, u32[]{:S(2)}, u32[]{:S(2)}) %collective-permute-start.6) | collective-permute-done | bytes 786464 | tf_op jit(solution)/shard_map/ppermute | solution.py:162
  90.7 1.9 collective-permute-start.10
  92.7 3.7 %collective-permute-done.4.rest_1_ = bf16[4,2,64,768]{3,2,1,0:T(8,128)(2,1)S(1)} collective-permute-done((bf16[4,2,64,768]{3,2,1,0:T(8,128)(2,1)S(1)}, bf16[4,2,64,768]{3,2,1,0:T(8,128)(2,1)S(1)}, u32[]{:S(2)}, u32[]{:S(2)}) %collective-permute-start.4) | collective-permute-done | bytes 786464 | tf_op jit(solution)/shard_map/ppermute | solution.py:162
  96.3 1.9 collective-permute-start.8
  98.3 2.4 collective-permute-start.9
  100.7 0.6 pad_add_fusion.where
  101.3 0.5 fusion
  101.8 0.8 pad_maximum_fusion.6
  102.7 0.9 copy-done.5
  103.6 0.3 copy-done.6
  103.8 0.9 copy-done.7
  104.7 0.6 broadcast_in_dim.7.docs_ref
  105.4 4.7 %kv_projection.1 = (bf16[264,256]{1,0:T(8,128)(2,1)}, bf16[256,4096]{1,0:T(8,128)(2,1)}) custom-call(s32[4]{0:T(128)} %pad_add_fusion.where, bf16[8,264,512]{2,1,0:T(8,128)(2,1)} %bitcast.34, bf16[8,256]{1,0:T(8,128)(2,1)} %broadcast_in_dim.7.docs_ref, f32[256,128]{1,0:T(8,128)} %get-tuple-element.30.cos_ref, f32[256,128]{1,0:T(8,128)} %get-tuple-element.31.sin_ref, ...), custom_call_target="tpu_custom_call" | custom-call | tf_op jit(solution)/shard_map/kv_projection/pallas_call | solution.py:181
  110.0 0.7 collective-permute-start.11
  110.7 0.9 broadcast_select_fusion
  111.7 1.3 collective-permute-start.12
  113.0 21.2 %collective-permute-start.13 = (bf16[264,256]{1,0:T(8,128)(2,1)S(1)}, bf16[264,256]{1,0:T(8,128)(2,1)S(1)}, u32[]{:S(2)}, u32[]{:S(2)}) collective-permute-start(bf16[264,256]{1,0:T(8,128)(2,1)S(1)} %get-tuple-element.18), channel_id=1, source_target_pairs={{0,128},{64,192},{256,384},{320,448},{384,256},{448,320},{1,129},{... | collective-permute-start | bytes 405512 | tf_op jit(solution)/shard_map/ppermute | solution.py:211
  134.2 6.2 %q_projection.1.q_ref = bf16[4,256,128]{2,1,0:T(8,128)(2,1)} custom-call(s32[4]{0:T(128)} %pad_add_fusion.where, bf16[256,4096]{1,0:T(8,128)(2,1)} %get-tuple-element.11.normed_ref, f32[256,128]{1,0:T(8,128)} %get-tuple-element.30.cos_ref, f32[256,128]{1,0:T(8,128)} %get-tuple-element.31.sin_ref, bf16[4,2,64,768]{3,2,1,0:T(8,128)(2,1)} %copy-done, ...), custom_call_target="tpu_custom_call" | custom-call | flops 1073741824 | bytes 6291456 | tf_op jit(solution)/shard_map/q_projection/pallas_call | solution.py:194
  140.6 1.9 collective-permute-start.14
  142.5 1.9 collective-permute-start.15
  144.5 3.9 %collective-permute-start.16 = (bf16[2,264,256]{2,1,0:T(8,128)(2,1)S(1)}, bf16[2,264,256]{2,1,0:T(8,128)(2,1)S(1)}, u32[]{:S(2)}, u32[]{:S(2)}) collective-permute-start(bf16[2,264,256]{2,1,0:T(8,128)(2,1)S(1)} %get-tuple-element.22), channel_id=1, source_target_pairs={{0,48},{16,0},{32,16},{48,32},{1,49},{17,1},{33,17},{49,33},{2,50}... | collective-permute-start | bytes 811016 | tf_op jit(solution)/shard_map/ppermute | solution.py:220
  148.4 3.5 %collective-permute-done.14 = bf16[2,264,256]{2,1,0:T(8,128)(2,1)S(1)} collective-permute-done((bf16[2,264,256]{2,1,0:T(8,128)(2,1)S(1)}, bf16[2,264,256]{2,1,0:T(8,128)(2,1)S(1)}, u32[]{:S(2)}, u32[]{:S(2)}) %collective-permute-start.14) | collective-permute-done | bytes 270368 | tf_op jit(solution)/shard_map/ppermute | solution.py:220
  151.9 3.3 %collective-permute-done.15 = bf16[2,264,256]{2,1,0:T(8,128)(2,1)S(1)} collective-permute-done((bf16[2,264,256]{2,1,0:T(8,128)(2,1)S(1)}, bf16[2,264,256]{2,1,0:T(8,128)(2,1)S(1)}, u32[]{:S(2)}, u32[]{:S(2)}) %collective-permute-start.15) | collective-permute-done | bytes 270368 | tf_op jit(solution)/shard_map/ppermute | solution.py:220
  155.2 4.0 %collective-permute-done.16 = bf16[2,264,256]{2,1,0:T(8,128)(2,1)S(1)} collective-permute-done((bf16[2,264,256]{2,1,0:T(8,128)(2,1)S(1)}, bf16[2,264,256]{2,1,0:T(8,128)(2,1)S(1)}, u32[]{:S(2)}, u32[]{:S(2)}) %collective-permute-start.16) | collective-permute-done | bytes 270368 | tf_op jit(solution)/shard_map/ppermute | solution.py:220
  159.4 2.1 collective-permute-start.17
  161.5 0.8 copy.8.docs_ref
  162.3 1.7 collective-permute-done.17.other_ref
  164.0 1.0 copy-done.9
  165.0 9.1 %attention.1.a_ref = bf16[256,512]{1,0:T(8,128)(2,1)} custom-call(bf16[4,256,128]{2,1,0:T(8,128)(2,1)} %q_projection.1.q_ref, f32[256,1]{1,0:T(8,128)} %copy.8.docs_ref, bf16[8,264,256]{2,1,0:T(8,128)(2,1)} %copy-done.1, bf16[8,264,256]{2,1,0:T(8,128)(2,1)} %copy-done.9), custom_call_target="tpu_custom_call" | custom-call | tf_op jit(solution)/shard_map/attention/pallas_call | solution.py:225
  174.0 4.1 %out_projection.1 = bf16[8,256,512]{2,1,0:T(8,128)(2,1)} custom-call(s32[1]{0:T(128)} %bitcast.zh, bf16[256,512]{1,0:T(8,128)(2,1)} %attention.1.a_ref, bf16[4,2,512,512]{3,2,1,0:T(8,128)(2,1)} %bitcast.33), custom_call_target="tpu_custom_call" | custom-call | tf_op jit(solution)/shard_map/out_projection/pallas_call | solution.py:234
  178.1 68.7 %reduce-scatter.2.cloned.1.call-done = bf16[256,512]{1,0:T(8,128)(2,1)} async-done(((bf16[2048,512]{1,0:T(8,128)(2,1)}), bf16[256,512]{1,0:T(8,128)(2,1)}) %reduce-scatter.2.cloned.1.call-update) | async-done | bytes 262160 | tf_op jit(solution)/shard_map/reduce_scatter | solution.py:248
  (57 shorter events, 0.6 us)
Async XLA Ops:
  6.5 24.3 %copy-start.10 = (bf16[64,512]{1,0:T(8,128)(2,1)S(1)}, bf16[64,512]{1,0:T(8,128)(2,1)}, u32[]{:S(2)}) copy-start(bf16[64,512]{1,0:T(8,128)(2,1)} %param.10) | copy-start | bytes 196612
  6.5 24.3 %copy-start.11 = (bf16[64,128]{1,0:T(8,128)(2,1)S(1)}, bf16[64,128]{1,0:T(8,128)(2,1)}, u32[]{:S(2)}) copy-start(bf16[64,128]{1,0:T(8,128)(2,1)} %param.11) | copy-start | bytes 49156
  6.5 24.4 %copy-start.12 = (bf16[64,128]{1,0:T(8,128)(2,1)S(1)}, bf16[64,128]{1,0:T(8,128)(2,1)}, u32[]{:S(2)}) copy-start(bf16[64,128]{1,0:T(8,128)(2,1)} %param.12) | copy-start | bytes 49156
  6.5 98.2 %all-gather.6.cloned.1.call-start = ((), (), s32[]{:S(2)}) async-start(), calls=%async_computation.3 | async-start | bytes 2433024 | tf_op jit(solution)/shard_map/all_gather | solution.py:155
  9.0 165.0 %all-gather.4.cloned.1.call-start = ((), (), s32[]{:S(2)}) async-start(), calls=%async_computation.1 | async-start | bytes 4325376 | tf_op jit(solution)/shard_map/all_gather | solution.py:168
  9.0 20.3 %collective-permute-start.18 = (bf16[64,512]{1,0:T(8,128)(2,1)}, bf16[64,512]{1,0:T(8,128)(2,1)S(1)}, u32[]{:S(2)}, u32[]{:S(2)}) collective-permute-start(bf16[64,512]{1,0:T(8,128)(2,1)} %bitcast.41), channel_id=1, source_target_pairs={{0,256},{256,0},{1,257},{257,1},{2,258},{258,2},{3,259},{259,3},{4... | collective-permute-start | bytes 196616 | tf_op jit(solution)/shard_map/ppermute | solution.py:165
  30.8 216.0 %reduce-scatter.2.cloned.1.call-start = ((), (), s32[]{:S(2)}) async-start(), calls=%async_computation.2 | async-start | bytes 2359296 | tf_op jit(solution)/shard_map/reduce_scatter | solution.py:248
  30.9 18.6 %collective-permute-start = (bf16[64,768]{1,0:T(8,128)(2,1)S(1)}, bf16[64,768]{1,0:T(8,128)(2,1)S(1)}, u32[]{:S(2)}, u32[]{:S(2)}) collective-permute-start(bf16[64,768]{1,0:T(8,128)(2,1)S(1)} %constant_dynamic-update-slice_fusion), channel_id=1, source_target_pairs={{0,256},{256,0},{1,257},{257,1},{2,258},{258,2},{3,259},{259,3},{4... | collective-permute-start | bytes 294920 | tf_op jit(solution)/shard_map/ppermute | solution.py:158
  49.6 9.2 %collective-permute-start.3 = (bf16[2,64,768]{2,1,0:T(8,128)(2,1)S(1)}, bf16[2,64,768]{2,1,0:T(8,128)(2,1)S(1)}, u32[]{:S(2)}, u32[]{:S(2)}) collective-permute-start(bf16[2,64,768]{2,1,0:T(8,128)(2,1)S(1)} %get-tuple-element.21), channel_id=1, source_target_pairs={{0,48},{8,200},{16,0},{24,216},{32,16},{40,232},{48,32},{56,248},{... | collective-permute-start | bytes 589832 | tf_op jit(solution)/shard_map/ppermute | solution.py:160
  52.3 7.6 %collective-permute-start.1 = (bf16[2,64,768]{2,1,0:T(8,128)(2,1)S(1)}, bf16[2,64,768]{2,1,0:T(8,128)(2,1)S(1)}, u32[]{:S(2)}, u32[]{:S(2)}) collective-permute-start(bf16[2,64,768]{2,1,0:T(8,128)(2,1)S(1)} %get-tuple-element.21), channel_id=1, source_target_pairs={{0,16},{8,72},{16,32},{24,88},{32,48},{40,104},{48,0},{56,120},{64... | collective-permute-start | bytes 589832 | tf_op jit(solution)/shard_map/ppermute | solution.py:160
  56.6 11.2 %collective-permute-start.2 = (bf16[2,64,768]{2,1,0:T(8,128)(2,1)S(1)}, bf16[2,64,768]{2,1,0:T(8,128)(2,1)S(1)}, u32[]{:S(2)}, u32[]{:S(2)}) collective-permute-start(bf16[2,64,768]{2,1,0:T(8,128)(2,1)S(1)} %get-tuple-element.21), channel_id=1, source_target_pairs={{0,32},{8,136},{16,48},{24,152},{32,0},{40,168},{48,16},{56,184},{... | collective-permute-start | bytes 589832 | tf_op jit(solution)/shard_map/ppermute | solution.py:160
  67.8 34.8 %copy-start.13 = (s32[256]{0:T(256)S(1)}, s32[256]{0:T(256)}, u32[]{:S(2)}) copy-start(s32[256]{0:T(256)} %param.9) | copy-start | bytes 3076
  67.9 37.4 %copy-start = (bf16[4,2,64,768]{3,2,1,0:T(8,128)(2,1)}, bf16[4,2,64,768]{3,2,1,0:T(8,128)(2,1)S(1)}, u32[]{:S(2)}) copy-start(bf16[4,2,64,768]{3,2,1,0:T(8,128)(2,1)S(1)} %pad_maximum_fusion.rest_0_) | copy-start | bytes 2359300
  67.9 22.8 %collective-permute-start.6 = (bf16[4,2,64,768]{3,2,1,0:T(8,128)(2,1)S(1)}, bf16[4,2,64,768]{3,2,1,0:T(8,128)(2,1)S(1)}, u32[]{:S(2)}, u32[]{:S(2)}) collective-permute-start(bf16[4,2,64,768]{3,2,1,0:T(8,128)(2,1)S(1)} %pad_maximum_fusion.rest_0_), channel_id=1, source_target_pairs={{0,192},{8,56},{16,208},{24,8},{32,224},{40,24},{48,240},{56,40},{... | collective-permute-start | bytes 2359304 | tf_op jit(solution)/shard_map/ppermute | solution.py:162
  72.8 23.5 %collective-permute-start.4 = (bf16[4,2,64,768]{3,2,1,0:T(8,128)(2,1)S(1)}, bf16[4,2,64,768]{3,2,1,0:T(8,128)(2,1)S(1)}, u32[]{:S(2)}, u32[]{:S(2)}) collective-permute-start(bf16[4,2,64,768]{3,2,1,0:T(8,128)(2,1)S(1)} %pad_maximum_fusion.rest_0_), channel_id=1, source_target_pairs={{0,64},{8,24},{16,80},{24,40},{32,96},{40,56},{48,112},{56,8},{64,... | collective-permute-start | bytes 2359304 | tf_op jit(solution)/shard_map/ppermute | solution.py:162
  74.7 23.5 %collective-permute-start.5 = (bf16[4,2,64,768]{3,2,1,0:T(8,128)(2,1)S(1)}, bf16[4,2,64,768]{3,2,1,0:T(8,128)(2,1)S(1)}, u32[]{:S(2)}, u32[]{:S(2)}) collective-permute-start(bf16[4,2,64,768]{3,2,1,0:T(8,128)(2,1)S(1)} %pad_maximum_fusion.rest_0_), channel_id=1, source_target_pairs={{0,128},{8,40},{16,144},{24,56},{32,160},{40,8},{48,176},{56,24},{... | collective-permute-start | bytes 2359304 | tf_op jit(solution)/shard_map/ppermute | solution.py:162
  78.9 23.8 %collective-permute-start.7 = (bf16[4,2,64,768]{3,2,1,0:T(8,128)(2,1)S(1)}, bf16[4,2,64,768]{3,2,1,0:T(8,128)(2,1)S(1)}, u32[]{:S(2)}, u32[]{:S(2)}) collective-permute-start(bf16[4,2,64,768]{3,2,1,0:T(8,128)(2,1)S(1)} %pad_maximum_fusion.rest_0_), channel_id=1, source_target_pairs={{0,8},{8,0},{1,9},{9,1},{2,10},{10,2},{3,11},{11,3},{4,12},{12,4},... | collective-permute-start | bytes 2359304 | tf_op jit(solution)/shard_map/ppermute | solution.py:167
  90.7 14.6 %copy-start.2 = (bf16[4,2,64,768]{3,2,1,0:T(8,128)(2,1)}, bf16[4,2,64,768]{3,2,1,0:T(8,128)(2,1)S(1)}, u32[]{:S(2)}) copy-start(bf16[4,2,64,768]{3,2,1,0:T(8,128)(2,1)S(1)} %collective-permute-done.6.rest_3_) | copy-start | bytes 2359300
  90.7 11.9 %collective-permute-start.10 = (bf16[4,2,64,768]{3,2,1,0:T(8,128)(2,1)S(1)}, bf16[4,2,64,768]{3,2,1,0:T(8,128)(2,1)S(1)}, u32[]{:S(2)}, u32[]{:S(2)}) collective-permute-start(bf16[4,2,64,768]{3,2,1,0:T(8,128)(2,1)S(1)} %collective-permute-done.6.rest_3_), channel_id=1, source_target_pairs={{0,8},{8,0},{1,9},{9,1},{2,10},{10,2},{3,11},{11,3},{4,12},{12,4},... | collective-permute-start | bytes 2359304 | tf_op jit(solution)/shard_map/ppermute | solution.py:167
  96.3 9.0 %copy-start.3 = (bf16[4,2,64,768]{3,2,1,0:T(8,128)(2,1)}, bf16[4,2,64,768]{3,2,1,0:T(8,128)(2,1)S(1)}, u32[]{:S(2)}) copy-start(bf16[4,2,64,768]{3,2,1,0:T(8,128)(2,1)S(1)} %collective-permute-done.4.rest_1_) | copy-start | bytes 2359300
  96.3 6.4 %collective-permute-start.8 = (bf16[4,2,64,768]{3,2,1,0:T(8,128)(2,1)S(1)}, bf16[4,2,64,768]{3,2,1,0:T(8,128)(2,1)S(1)}, u32[]{:S(2)}, u32[]{:S(2)}) collective-permute-start(bf16[4,2,64,768]{3,2,1,0:T(8,128)(2,1)S(1)} %collective-permute-done.4.rest_1_), channel_id=1, source_target_pairs={{0,8},{8,0},{1,9},{9,1},{2,10},{10,2},{3,11},{11,3},{4,12},{12,4},... | collective-permute-start | bytes 2359304 | tf_op jit(solution)/shard_map/ppermute | solution.py:167
  98.2 7.1 %copy-start.4 = (bf16[4,2,64,768]{3,2,1,0:T(8,128)(2,1)}, bf16[4,2,64,768]{3,2,1,0:T(8,128)(2,1)S(1)}, u32[]{:S(2)}) copy-start(bf16[4,2,64,768]{3,2,1,0:T(8,128)(2,1)S(1)} %collective-permute-done.5.rest_2_) | copy-start | bytes 2359300
  98.3 6.5 %collective-permute-start.9 = (bf16[4,2,64,768]{3,2,1,0:T(8,128)(2,1)S(1)}, bf16[4,2,64,768]{3,2,1,0:T(8,128)(2,1)}, u32[]{:S(2)}, u32[]{:S(2)}) collective-permute-start(bf16[4,2,64,768]{3,2,1,0:T(8,128)(2,1)S(1)} %collective-permute-done.5.rest_2_), channel_id=1, source_target_pairs={{0,8},{8,0},{1,9},{9,1},{2,10},{10,2},{3,11},{11,3},{4,12},{12,4},... | collective-permute-start | bytes 2359304 | tf_op jit(solution)/shard_map/ppermute | solution.py:167
  102.7 0.9 copy-start.5
  102.7 1.1 copy-start.6
  103.8 0.9 copy-start.7
  110.0 0.7 collective-permute-start.11
  111.7 28.8 %collective-permute-start.12 = (bf16[264,256]{1,0:T(8,128)(2,1)S(1)}, bf16[264,256]{1,0:T(8,128)(2,1)S(1)}, u32[]{:S(2)}, u32[]{:S(2)}) collective-permute-start(bf16[264,256]{1,0:T(8,128)(2,1)S(1)} %get-tuple-element.19), channel_id=1, source_target_pairs={{0,64},{64,128},{128,192},{256,320},{320,384},{384,448},{448,256},... | collective-permute-start | bytes 405512 | tf_op jit(solution)/shard_map/ppermute | solution.py:213
  113.0 27.5 %collective-permute-start.13 = (bf16[264,256]{1,0:T(8,128)(2,1)S(1)}, bf16[264,256]{1,0:T(8,128)(2,1)S(1)}, u32[]{:S(2)}, u32[]{:S(2)}) collective-permute-start(bf16[264,256]{1,0:T(8,128)(2,1)S(1)} %get-tuple-element.18), channel_id=1, source_target_pairs={{0,128},{64,192},{256,384},{320,448},{384,256},{448,320},{1,129},{... | collective-permute-start | bytes 405512 | tf_op jit(solution)/shard_map/ppermute | solution.py:211
  134.2 6.3 %copy-start.8 = (bf16[264,256]{1,0:T(8,128)(2,1)S(1)}, bf16[264,256]{1,0:T(8,128)(2,1)}, u32[]{:S(2)}) copy-start(bf16[264,256]{1,0:T(8,128)(2,1)} %get-tuple-element.10) | copy-start | bytes 405508
  140.6 11.2 %collective-permute-start.14 = (bf16[2,264,256]{2,1,0:T(8,128)(2,1)S(1)}, bf16[2,264,256]{2,1,0:T(8,128)(2,1)S(1)}, u32[]{:S(2)}, u32[]{:S(2)}) collective-permute-start(bf16[2,264,256]{2,1,0:T(8,128)(2,1)S(1)} %get-tuple-element.24), channel_id=1, source_target_pairs={{0,16},{16,32},{32,48},{48,0},{1,17},{17,33},{33,49},{49,1},{2,18}... | collective-permute-start | bytes 811016 | tf_op jit(solution)/shard_map/ppermute | solution.py:220
  142.5 12.7 %collective-permute-start.15 = (bf16[2,264,256]{2,1,0:T(8,128)(2,1)S(1)}, bf16[2,264,256]{2,1,0:T(8,128)(2,1)S(1)}, u32[]{:S(2)}, u32[]{:S(2)}) collective-permute-start(bf16[2,264,256]{2,1,0:T(8,128)(2,1)S(1)} %get-tuple-element.23), channel_id=1, source_target_pairs={{0,32},{16,48},{32,0},{48,16},{1,33},{17,49},{33,1},{49,17},{2,34}... | collective-permute-start | bytes 811016 | tf_op jit(solution)/shard_map/ppermute | solution.py:220
  144.5 14.7 %collective-permute-start.16 = (bf16[2,264,256]{2,1,0:T(8,128)(2,1)S(1)}, bf16[2,264,256]{2,1,0:T(8,128)(2,1)S(1)}, u32[]{:S(2)}, u32[]{:S(2)}) collective-permute-start(bf16[2,264,256]{2,1,0:T(8,128)(2,1)S(1)} %get-tuple-element.22), channel_id=1, source_target_pairs={{0,48},{16,0},{32,16},{48,32},{1,49},{17,1},{33,17},{49,33},{2,50}... | collective-permute-start | bytes 811016 | tf_op jit(solution)/shard_map/ppermute | solution.py:220
  159.4 4.6 %collective-permute-start.17 = (bf16[8,264,256]{2,1,0:T(8,128)(2,1)S(1)}, bf16[8,264,256]{2,1,0:T(8,128)(2,1)S(1)}, u32[]{:S(2)}, u32[]{:S(2)}) collective-permute-start(bf16[8,264,256]{2,1,0:T(8,128)(2,1)S(1)} %bitcast_dynamic-update-slice_fusion), channel_id=1, source_target_pairs={{0,8},{8,0},{1,9},{9,1},{2,10},{10,2},{3,11},{11,3},{4,12},{12,4},... | collective-permute-start | bytes 3244040 | tf_op jit(solution)/shard_map/ppermute | solution.py:222
  162.3 1.7 copy-start.1
  164.0 1.0 copy-start.9
Sparse Core Ops, SparseCore 0:
  9.4 73.9 all-gather.5
  86.6 61.1 all-gather.3
  178.2 68.5 reduce-scatter.1
